TPU v7x, 32 devices: a whole 2x2x4 slice. The times are simulated.
32 devices in a mesh: dp: 8 (over z, x), mix: 4 (over y, core).
Axes of the slice: x: 2, y: 2, z: 4, core: 2. Of those that a mesh axis runs over, the one named last changes fastest.
Arguments:
- inputs: bfloat16 [40, 1280, 768], P('dp', 'mix'), may hold values from -6 to 6
- pass_count: int32 [40], P('dp'), may hold values from 2 to 5
- pass_embed: bfloat16 [5, 768], replicated, may hold values from -3 to 3
- ln1_gain: bfloat16 [768], replicated, may hold values from 0.5 to 1.5
- ln1_bias: bfloat16 [768], replicated, may hold values from -0.59765625 to 0.59765625
- w_qkv: bfloat16 [768, 2304], replicated, may hold values from -0.21875 to 0.21875
- bias_q: bfloat16 [768], replicated, may hold values from -0.59765625 to 0.59765625
- bias_v: bfloat16 [768], replicated, may hold values from -0.29882812 to 0.29882812
- w_out: bfloat16 [768, 768], replicated, may hold values from -3.5 to 3.5
- bias_out: bfloat16 [768], replicated, may hold values from -0.59765625 to 0.59765625
- ln2_gain: bfloat16 [768], replicated, may hold values from 0.5 to 1.5
- ln2_bias: bfloat16 [768], replicated, may hold values from -0.59765625 to 0.59765625
- w_up: bfloat16 [768, 3072], replicated, may hold values from -0.21875 to 0.21875
- bias_up: bfloat16 [3072], replicated, may hold values from -0.59765625 to 0.59765625
- w_down: bfloat16 [3072, 768], replicated, may hold values from -0.21875 to 0.21875
- bias_down: bfloat16 [768], replicated, may hold values from -0.59765625 to 0.59765625
- cotangent: bfloat16 [40, 1280, 768], P('dp', 'mix'), may hold values from -6 to 6
Outputs:
- out: float32 [40, 1280, 768], P('dp', 'mix')
- grad_x: float32 [40, 1280, 768], P('dp', 'mix')
- grad_pass_embed: float32 [5, 768], replicated
- grad_ln1_gain: float32 [768], replicated
- grad_ln1_bias: float32 [768], replicated
- grad_w_qkv: float32 [768, 2304], P('dp', 'mix')
- grad_bias_q: float32 [768], replicated
- grad_bias_v: float32 [768], replicated
- grad_w_out: float32 [768, 768], P('dp', 'mix')
- grad_bias_out: float32 [768], replicated
- grad_ln2_gain: float32 [768], replicated
- grad_ln2_bias: float32 [768], replicated
- grad_w_up: float32 [768, 3072], P('dp', 'mix')
- grad_bias_up: float32 [3072], replicated
- grad_w_down: float32 [3072, 768], P('dp', 'mix')
- grad_bias_down: float32 [768], replicated
Inputs may be any that keep to these rules, and one draw needn't show every extreme that they name: Item i uses passes 0 to pass_count[i] - 1 of each token; the other slots are masked.
All inputs are finite; a program needn't handle non-finite values.
Results may differ from a plain program's by a relative error of at most 0.0095.
Values may be sent and summed in bfloat16 or wider, within the bound.
No kernel may reach another device: no remote copies, remote signals or barrier semaphores. Data moves between devices by JAX's collectives and lax.ppermute only.
A program may use at most 256 MiB of HBM per device.

v0:
```python
from functools import partial
import math

import jax
import jax.numpy as jnp
from jax import lax
from jax.sharding import PartitionSpec as P

HEAD = 64
PASSES = 5


epsilon = 1e-05
highest = lax.Precision.HIGHEST


def norm_forward(values, gain_vec, shift_vec):
    center = values - jnp.mean(values, axis=-1, keepdims=True)
    inverse = lax.rsqrt(jnp.mean(center * center, axis=-1, keepdims=True) + epsilon)
    normed = center * inverse
    return (normed * gain_vec + shift_vec, normed, inverse)


def norm_backward(upstream, normed, inverse, gain_vec):
    scaled = upstream * gain_vec
    inner_term = scaled - jnp.mean(scaled, axis=-1, keepdims=True)
    inner_term = inner_term - normed * jnp.mean(scaled * normed, axis=-1, keepdims=True)
    return (inverse * inner_term, jnp.sum(upstream * normed, axis=0), jnp.sum(upstream, axis=0))


def split_parts(stacked):
    slot_total = stacked.shape[0]
    heads_dev = stacked.shape[-1] // HEAD
    queries = stacked[:, 0].reshape(slot_total, heads_dev, HEAD)
    key_rows = stacked[:, 1].reshape(slot_total, heads_dev, HEAD)
    value_rows = stacked[:, 2].reshape(slot_total, heads_dev, HEAD)
    return (queries, key_rows, value_rows)


def score_table(queries, key_rows, passes_item):
    slot_total = key_rows.shape[0]
    raw_scores = jnp.einsum("qhd,khd->hqk", queries, key_rows, preferred_element_type=jnp.float32)
    raw_scores = raw_scores * (1.0 / math.sqrt(HEAD))
    slot_ids = lax.iota(jnp.int32, slot_total)
    allowed = (slot_ids[None, :] <= slot_ids[:, None]) & (slot_ids[None, :] % PASSES < passes_item)
    return jnp.where(allowed[None], raw_scores, -1e30)


def attend_item(pieces):
    stacked, passes_item = pieces
    queries, key_rows, value_rows = split_parts(stacked)
    scores = score_table(queries, key_rows, passes_item)
    row_max = jnp.max(scores, axis=-1, keepdims=True)
    log_total = row_max + jnp.log(jnp.sum(jnp.exp(scores - row_max), axis=-1, keepdims=True))
    weights_low = jnp.exp(scores - log_total).astype(jnp.bfloat16)
    attended = jnp.einsum(
        "hqk,khd->qhd", weights_low, value_rows, preferred_element_type=jnp.float32
    )
    return (attended.reshape(stacked.shape[0], -1).astype(jnp.bfloat16), log_total)


def attend_back(pieces):
    stacked, grad_heads, log_total, passes_item = pieces
    queries, key_rows, value_rows = split_parts(stacked)
    slot_total = stacked.shape[0]
    scores = score_table(queries, key_rows, passes_item)
    probs = jnp.exp(scores - log_total)
    grad_part = grad_heads.reshape(slot_total, -1, HEAD)
    grad_probs = jnp.einsum(
        "qhd,khd->hqk", grad_part, value_rows, preferred_element_type=jnp.float32
    )
    row_inner = jnp.sum(probs * grad_probs, axis=-1, keepdims=True)
    grad_scores = (probs * (grad_probs - row_inner)).astype(jnp.bfloat16)
    score_scale = 1.0 / math.sqrt(HEAD)
    grad_query = (
        jnp.einsum("hqk,khd->qhd", grad_scores, key_rows, preferred_element_type=jnp.float32)
        * score_scale
    )
    grad_key = (
        jnp.einsum("hqk,qhd->khd", grad_scores, queries, preferred_element_type=jnp.float32)
        * score_scale
    )
    grad_value = jnp.einsum(
        "hqk,qhd->khd", probs.astype(jnp.bfloat16), grad_part, preferred_element_type=jnp.float32
    )
    joined = jnp.stack([grad_query, grad_key, grad_value], axis=1).astype(jnp.bfloat16)
    return joined.reshape(slot_total, 3, -1)


def per_device(
    inputs,
    pass_count,
    pass_embed,
    ln1_gain,
    ln1_bias,
    w_qkv,
    bias_q,
    bias_v,
    w_out,
    bias_out,
    ln2_gain,
    ln2_bias,
    w_up,
    bias_up,
    w_down,
    bias_down,
    cotangent,
):
    item_dev, slot_dev, model_width = inputs.shape
    row_total = item_dev * slot_dev
    slot_ids = lax.axis_index("mix") * slot_dev + lax.iota(jnp.int32, slot_dev)
    pass_ids = slot_ids % PASSES
    onehot = (pass_ids[:, None] == lax.iota(jnp.int32, PASSES)[None, :]).astype(jnp.float32)
    keep_mask = (pass_ids[None, :] < pass_count[:, None]).astype(jnp.float32).reshape(row_total, 1)
    pass_rows = jnp.dot(onehot, pass_embed.astype(jnp.float32), precision=highest)
    hidden = (inputs.astype(jnp.float32) + pass_rows[None]).reshape(row_total, model_width)
    gain_one = ln1_gain.astype(jnp.float32)
    gain_two = ln2_gain.astype(jnp.float32)
    first, normed_one, inverse_one = norm_forward(hidden, gain_one, ln1_bias.astype(jnp.float32))
    first_low = first.astype(jnp.bfloat16)
    joined_bias = jnp.concatenate(
        [
            bias_q.astype(jnp.float32),
            jnp.zeros((model_width,), jnp.float32),
            bias_v.astype(jnp.float32),
        ]
    )
    joined = jnp.dot(first_low, w_qkv, preferred_element_type=jnp.float32) + joined_bias
    head_block = lax.all_to_all(
        joined.astype(jnp.bfloat16).reshape(item_dev, slot_dev, 3, model_width),
        "mix",
        split_axis=3,
        concat_axis=1,
        tiled=True,
    )
    attended_heads, log_totals = lax.map(attend_item, (head_block, pass_count))
    attended = lax.all_to_all(
        attended_heads, "mix", split_axis=1, concat_axis=2, tiled=True
    ).reshape(row_total, model_width)
    attn_out = jnp.dot(attended, w_out, preferred_element_type=jnp.float32) + bias_out.astype(
        jnp.float32
    )
    mixed_rows = hidden + keep_mask * attn_out
    second, normed_two, inverse_two = norm_forward(
        mixed_rows, gain_two, ln2_bias.astype(jnp.float32)
    )
    second_low = second.astype(jnp.bfloat16)
    pre_act = jnp.dot(second_low, w_up, preferred_element_type=jnp.float32) + bias_up.astype(
        jnp.float32
    )
    act_low = jax.nn.gelu(pre_act, approximate=True).astype(jnp.bfloat16)
    result = mixed_rows + keep_mask * (
        jnp.dot(act_low, w_down, preferred_element_type=jnp.float32) + bias_down.astype(jnp.float32)
    )
    grad_top = cotangent.astype(jnp.float32).reshape(row_total, model_width)
    grad_mlp = (keep_mask * grad_top).astype(jnp.bfloat16)
    grad_wdown = jnp.dot(act_low.T, grad_mlp, preferred_element_type=jnp.float32)
    grad_bdown = jnp.sum(grad_mlp, axis=0, dtype=jnp.float32)
    unused_out, gelu_back = jax.vjp(partial(jax.nn.gelu, approximate=True), pre_act)
    grad_pre = gelu_back(jnp.dot(grad_mlp, w_down.T, preferred_element_type=jnp.float32))[0].astype(
        jnp.bfloat16
    )
    grad_wup = jnp.dot(second_low.T, grad_pre, preferred_element_type=jnp.float32)
    grad_bup = jnp.sum(grad_pre, axis=0, dtype=jnp.float32)
    grad_norm_two, grad_gain_two, grad_shift_two = norm_backward(
        jnp.dot(grad_pre, w_up.T, preferred_element_type=jnp.float32),
        normed_two,
        inverse_two,
        gain_two,
    )
    grad_mixed = grad_top + grad_norm_two
    grad_attn = (keep_mask * grad_mixed).astype(jnp.bfloat16)
    grad_wout = jnp.dot(attended.T, grad_attn, preferred_element_type=jnp.float32)
    grad_bout = jnp.sum(grad_attn, axis=0, dtype=jnp.float32)
    grad_attended = jnp.dot(grad_attn, w_out.T, preferred_element_type=jnp.float32).astype(
        jnp.bfloat16
    )
    grad_attended = grad_attended.reshape(item_dev, slot_dev, model_width)
    grad_heads = lax.all_to_all(grad_attended, "mix", split_axis=2, concat_axis=1, tiled=True)
    grad_stacked = lax.map(attend_back, (head_block, grad_heads, log_totals, pass_count))
    grad_joined = lax.all_to_all(
        grad_stacked, "mix", split_axis=1, concat_axis=3, tiled=True
    ).reshape(row_total, 3 * model_width)
    grad_wqkv = jnp.dot(first_low.T, grad_joined, preferred_element_type=jnp.float32)
    grad_bq = jnp.sum(grad_joined[:, :model_width], axis=0, dtype=jnp.float32)
    grad_bv = jnp.sum(grad_joined[:, 2 * model_width :], axis=0, dtype=jnp.float32)
    grad_norm_one, grad_gain_one, grad_shift_one = norm_backward(
        jnp.dot(grad_joined, w_qkv.T, preferred_element_type=jnp.float32),
        normed_one,
        inverse_one,
        gain_one,
    )
    grad_hidden = grad_mixed + grad_norm_one
    grad_embed = jnp.dot(
        onehot.T,
        jnp.sum(grad_hidden.reshape(item_dev, slot_dev, model_width), axis=0),
        precision=highest,
    )
    partial_sums = (
        lax.psum_scatter(grad_wqkv, "dp", scatter_dimension=0, tiled=True),
        lax.psum_scatter(grad_wout, "dp", scatter_dimension=0, tiled=True),
        lax.psum_scatter(grad_wup, "dp", scatter_dimension=0, tiled=True),
        lax.psum_scatter(grad_wdown, "dp", scatter_dimension=0, tiled=True),
    )
    reduced = (
        lax.psum_scatter(partial_sums[0], "mix", scatter_dimension=1, tiled=True),
        lax.psum_scatter(partial_sums[1], "mix", scatter_dimension=1, tiled=True),
        lax.psum_scatter(partial_sums[2], "mix", scatter_dimension=1, tiled=True),
        lax.psum_scatter(partial_sums[3], "mix", scatter_dimension=1, tiled=True),
    )
    smalls = lax.psum(
        (
            grad_embed,
            grad_gain_one,
            grad_shift_one,
            grad_bq,
            grad_bv,
            grad_bout,
            grad_gain_two,
            grad_shift_two,
            grad_bup,
            grad_bdown,
        ),
        ("dp", "mix"),
    )
    return (
        result.reshape(item_dev, slot_dev, model_width),
        grad_hidden.reshape(item_dev, slot_dev, model_width),
        smalls[0],
        smalls[1],
        smalls[2],
        reduced[0],
        smalls[3],
        smalls[4],
        reduced[1],
        smalls[5],
        smalls[6],
        smalls[7],
        reduced[2],
        smalls[8],
        reduced[3],
        smalls[9],
    )


def solution(mesh):
    return jax.shard_map(
        per_device,
        mesh=mesh,
        in_specs=(
            P("dp", "mix", None),
            P("dp"),
            P(),
            P(),
            P(),
            P(),
            P(),
            P(),
            P(),
            P(),
            P(),
            P(),
            P(),
            P(),
            P(),
            P(),
            P("dp", "mix", None),
        ),
        out_specs=(
            P("dp", "mix", None),
            P("dp", "mix", None),
            P(),
            P(),
            P(),
            P("dp", "mix"),
            P(),
            P(),
            P("dp", "mix"),
            P(),
            P(),
            P(),
            P("dp", "mix"),
            P(),
            P("dp", "mix"),
            P(),
        ),
        check_vma=False,
    )
```

profile of v0, /device:TPU:0, one launch (start us, length us, event | category | flops | bytes accessed | tf_op | source)
XLA Modules:
  0.0 1744.5 jit_solution(5274464120580839720)
XLA Ops:
  39.8 16.9 reshape.398
  56.7 23.4 %copy.79 = bf16[5,320,3,768]{1,2,0,3:T(4,128)(2,1)} copy(bf16[5,320,3,768]{3,2,1,0:T(4,128)(2,1)} %reshape.398) | data formatting | bytes 14745600 | tf_op jit(solution)/shard_map/reshape | solution.py:130
  86.3 130.4 %all-to-all-done = bf16[5,320,3,768]{1,2,0,3:T(4,128)(2,1)} async-done(((bf16[5,320,3,768]{1,2,0,3:T(4,128)(2,1)}), bf16[5,320,3,768]{1,2,0,3:T(4,128)(2,1)}, u32[]{:S(2)}, u32[]{:S(2)}) %all-to-all-start) | async-done | bytes 7372832 | tf_op jit(solution)/shard_map/all_to_all | solution.py:129
  226.0 14.7 copy.81
  240.7 14.7 all_to_all.51
  255.4 182.3 %while.26 = (s32[]{:T(128)}, bf16[5,1280,192]{1,2,0:T(8,128)(2,1)}, f32[5,3,1280,1]{2,1,3,0:T(4,128)}, bf16[5,1280,3,192]{1,3,2,0:T(8,128)(2,1)}, s32[5]{0:T(128)S(1)}, /*index=5*/s32[]{:T(128)}) while((s32[]{:T(128)}, bf16[5,1280,192]{1,2,0:T(8,128)(2,1)}, f32[5,3,1280,1]{2,1,3,0:T(4,128)}, bf16[5,1280,3,192]{1,3,2,0:T(8,128)(2,1)}, ...), condition=%wide.region_5.6_spmd, body=%wide.region_2.5_spmd.sunk | while | flops 1296225280 | bytes 71247464 | solution.py:136
  270.2 9.8 exponential_reduce_fusion.2
  281.4 9.9 fusion.116
  317.8 9.9 fusion.116
  343.1 9.8 exponential_reduce_fusion.2
  354.2 9.9 fusion.116
  390.6 9.9 fusion.116
  427.0 9.9 fusion.116
  465.4 21.5 %all-to-all-done.1 = bf16[4,2,153600]{2,1,0:T(2,128)(2,1)} async-done(((bf16[4,2,153600]{2,1,0:T(2,128)(2,1)}), bf16[4,2,153600]{2,1,0:T(2,128)(2,1)}, u32[]{:S(2)}, u32[]{:S(2)}) %all-to-all-start.1) | async-done | bytes 2457632 | tf_op jit(solution)/shard_map/all_to_all | solution.py:137
  514.5 19.6 %multiply_convert_fusion.1 = (bf16[1600,3072]{1,0:T(8,128)(2,1)}, f32[1600,3072]{1,0:T(8,128)}) fusion(f32[3072]{0:T(1024)S(1)} %copy-done.29, bf16[768,3072]{1,0:T(8,128)(2,1)} %param.33, f32[1600,768]{1,0:T(8,128)S(1)} %get-tuple-element.304, f32[768]{0:T(1024)S(1)} %copy-done.30, f32[768]{0:T(1024)S(1)} %copy-done.28, f32[1600]{0:T(1024)S(1)} %add_rsqrt_fusion.1, ...), kind=kOutput, calls=%fused_computation.53 | convolution fusion | flops 7605043200 | bytes 39156224 | tf_op jit(solution)/shard_map/dot_general | solution.py:148
  534.0 24.4 %convert_reduce_fusion = (f32[3072]{0:T(1024)}, bf16[1600,3072]{1,0:T(8,128)(2,1)}) fusion(f32[1600,3072]{1,0:T(8,128)} %get-tuple-element.306, f32[3072]{0:T(1024)S(1)} %copy-done.29, bf16[1600,768]{1,0:T(8,128)(2,1)S(1)} %copy-done.7, bf16[3072,768]{1,0:T(8,128)(2,1)} %param.35), kind=kOutput, calls=%fused_computation.52 | convolution fusion | flops 7662793728 | bytes 36691968 | tf_op jit(solution)/shard_map/dot_general | solution.py:160
  558.5 15.0 multiply_reduce_fusion.1
  593.9 53.8 %all-to-all-done.2 = bf16[5,320,768]{1,0,2:T(8,128)(2,1)} async-done(((bf16[5,320,768]{1,0,2:T(8,128)(2,1)}), bf16[5,320,768]{1,0,2:T(8,128)(2,1)}, u32[]{:S(2)}, u32[]{:S(2)}) %all-to-all-start.2) | async-done | bytes 2457632 | tf_op jit(solution)/shard_map/all_to_all | solution.py:179
  660.1 286.4 %while.27 = (s32[]{:T(128)}, bf16[5,1280,3,192]{1,3,2,0:T(8,128)(2,1)}, bf16[5,1280,3,192]{1,3,2,0:T(8,128)(2,1)}, s32[5]{0:T(128)S(1)}, f32[5,3,1280,1]{2,1,3,0...) while((s32[]{:T(128)}, bf16[5,1280,3,192]{1,3,2,0:T(8,128)(2,1)}, ...), condition=%wide.region_12.13_spmd, body=%wide.region_10.12_spmd.sunk | while | flops 3198899200 | bytes 167523984 | solution.py:180
  675.1 10.5 fusion.130
  685.6 12.3 multiply_reduce_fusion.10
  698.0 13.2 multiply_convert_fusion.5
  732.4 10.5 fusion.130
  742.9 12.3 multiply_reduce_fusion.10
  755.2 13.2 multiply_convert_fusion.5
  789.7 10.5 fusion.130
  800.2 12.3 multiply_reduce_fusion.10
  812.5 13.2 multiply_convert_fusion.5
  846.9 10.5 fusion.130
  857.4 12.3 multiply_reduce_fusion.10
  869.8 13.2 multiply_convert_fusion.5
  904.2 10.5 fusion.130
  914.7 12.3 multiply_reduce_fusion.10
  927.0 13.2 multiply_convert_fusion.5
  946.5 19.2 %copy.87 = bf16[5,1280,3,192]{3,2,0,1:T(4,128)(2,1)} copy(bf16[5,1280,3,192]{1,3,2,0:T(8,128)(2,1)} %get-tuple-element.163) | data formatting | bytes 14745600 | tf_op jit(solution)/shard_map/while | solution.py:180
  978.6 137.2 %all-to-all-done.3 = bf16[5,1280,3,192]{3,2,0,1:T(4,128)(2,1)} async-done(((bf16[5,1280,3,192]{3,2,0,1:T(4,128)(2,1)}), bf16[5,1280,3,192]{3,2,0,1:T(4,128)(2,1)}, u32[]{:S(2)}, u32[]{:S(2)}) %all-to-all-start.3) | async-done | bytes 7372832 | tf_op jit(solution)/shard_map/all_to_all | solution.py:181
  1115.8 24.6 %copy.103 = bf16[5,4,320,3,192]{4,1,3,2,0:T(4,128)(2,1)} copy(bf16[5,4,320,3,192]{4,3,0,2,1:T(4,128)(2,1)} %bitcast.32) | data formatting | bytes 14745600 | tf_op jit(solution)/shard_map/all_to_all | solution.py:181
  1140.4 16.9 reshape.403
  1157.3 12.1 fusion.47
  1169.7 14.4 fusion.49
  1186.2 16.1 fusion.41
  1202.4 97.4 %reduce-scatter.15.cloned.1.call-done = f32[96,2304]{1,0:T(8,128)} async-done(((f32[768,2304]{1,0:T(8,128)}), f32[96,2304]{1,0:T(8,128)}) %reduce-scatter.15.cloned.1.call-update) | async-done | bytes 884752 | tf_op jit(solution)/shard_map/reduce_scatter | solution.py:200
  1302.5 162.2 %reduce-scatter.23.cloned.1.call-done = f32[384,768]{1,0:T(8,128)} async-done(((f32[3072,768]{1,0:T(8,128)}), f32[384,768]{1,0:T(8,128)}) %reduce-scatter.23.cloned.1.call-update) | async-done | bytes 1179664 | tf_op jit(solution)/shard_map/reduce_scatter | solution.py:203
  1470.4 14.4 multiply_add_fusion.1
  1488.6 164.0 %reduce-scatter.19.cloned.1.call-done = f32[96,3072]{1,0:T(8,128)} async-done(((f32[768,3072]{1,0:T(8,128)}), f32[96,3072]{1,0:T(8,128)}) %reduce-scatter.19.cloned.1.call-update) | async-done | bytes 1179664 | tf_op jit(solution)/shard_map/reduce_scatter | solution.py:202
  1652.6 14.2 multiply_reduce_fusion.2
  1682.4 41.3 %all-reduce = (f32[5,768]{1,0:T(8,128)}, f32[768]{0:T(1024)}, f32[768]{0:T(1024)}, f32[768]{0:T(1024)}, f32[768]{0:T(1024)}, /*index=5*/f32[768]{0:T(1024)}, f32...) all-reduce(f32[5,768]{1,0:T(8,128)} %fusion.34, ...), channel_id=1, replica_groups=mesh['dp'=8,'mix'=4] {'dp','mix'}, use_global_device_ids=true, to_apply=%region_16.17 | all-reduce | flops 13056 | bytes 104448 | tf_op jit(solution)/shard_map/psum | solution.py:211
  1725.6 11.7 reduce-scatter.21.cloned.1.call-done
  (262 shorter events, 399.5 us)
Async XLA Ops:
  7.2 24.1 %copy-start = (bf16[768,2304]{1,0:T(8,128)(2,1)S(1)}, bf16[768,2304]{1,0:T(8,128)(2,1)}, u32[]{:S(2)}) copy-start(bf16[768,2304]{1,0:T(8,128)(2,1)} %param.26) | copy-start | bytes 10616836
  16.8 12.4 copy-start.13
  22.6 6.5 copy-start.25
  22.6 6.5 copy-start.26
  22.6 8.7 copy-start.15
  22.6 8.7 copy-start.17
  22.6 8.7 copy-start.24
  29.1 2.2 copy-start.3
  80.1 136.6 %all-to-all-start = ((bf16[5,320,3,768]{1,2,0,3:T(4,128)(2,1)}), bf16[5,320,3,768]{1,2,0,3:T(4,128)(2,1)}, u32[]{:S(2)}, u32[]{:S(2)}) async-start(bf16[5,320,3,768]{1,2,0,3:T(4,128)(2,1)} %copy.79), calls=%async_computation | async-start | bytes 23592960 | tf_op jit(solution)/shard_map/all_to_all | solution.py:129
  240.7 14.8 copy-start.35
  445.1 12.1 copy-start.32
  445.1 12.7 copy-start.33
  445.1 13.3 copy-start.34
  445.1 13.9 copy-start.22
  452.3 34.5 %all-to-all-start.1 = ((bf16[4,2,153600]{2,1,0:T(2,128)(2,1)}), bf16[4,2,153600]{2,1,0:T(2,128)(2,1)}, u32[]{:S(2)}, u32[]{:S(2)}) async-start(bf16[4,2,153600]{2,1,0:T(2,128)(2,1)} %reshape.412), calls=%async_computation.1 | async-start | bytes 4915200 | tf_op jit(solution)/shard_map/all_to_all | solution.py:137
  459.8 34.3 %copy-start.8 = (f32[5,320]{1,0:T(8,128)}, f32[5,320]{1,0:T(8,128)S(1)}, u32[]{:S(2)}) copy-start(f32[5,320]{1,0:T(8,128)S(1)} %compare_convert_fusion) | copy-start | bytes 19204
  501.1 6.6 copy-start.10
  501.1 6.6 copy-start.31
  513.7 59.8 %copy-start.4 = (f32[1600,768]{1,0:T(8,128)}, f32[1600,768]{1,0:T(8,128)S(1)}, u32[]{:S(2)}) copy-start(f32[1600,768]{1,0:T(8,128)S(1)} %get-tuple-element.304) | copy-start | bytes 14745604
  513.7 59.8 %copy-start.11 = (f32[1600]{0:T(1024)}, f32[1600]{0:T(1024)S(1)}, u32[]{:S(2)}) copy-start(f32[1600]{0:T(1024)S(1)} %broadcast_multiply_fusion.5) | copy-start | bytes 19204
  514.5 59.0 %copy-start.19 = (f32[1600]{0:T(1024)}, f32[1600]{0:T(1024)S(1)}, u32[]{:S(2)}) copy-start(f32[1600]{0:T(1024)S(1)} %add_rsqrt_fusion.1) | copy-start | bytes 19204
  514.5 19.6 %copy-start.7 = (bf16[1600,768]{1,0:T(8,128)(2,1)S(1)}, bf16[1600,768]{1,0:T(8,128)(2,1)}, u32[]{:S(2)}) copy-start(bf16[1600,768]{1,0:T(8,128)(2,1)} %fusion.28) | copy-start | bytes 7372804
  558.5 15.0 copy-start.2
  573.5 5.4 copy-start.37
  578.9 3.6 copy-start.6
  588.9 58.8 %all-to-all-start.2 = ((bf16[5,320,768]{1,0,2:T(8,128)(2,1)}), bf16[5,320,768]{1,0,2:T(8,128)(2,1)}, u32[]{:S(2)}, u32[]{:S(2)}) async-start(bf16[5,320,768]{1,0,2:T(8,128)(2,1)} %copy.84), calls=%async_computation.2 | async-start | bytes 9437184 | tf_op jit(solution)/shard_map/all_to_all | solution.py:179
  647.7 12.4 copy-start.36
  713.0 3.1 copy-start.1
  770.3 3.1 copy-start.1
  827.6 3.1 copy-start.1
  884.8 3.1 copy-start.1
  942.1 3.1 copy-start.1
  965.7 150.1 %all-to-all-start.3 = ((bf16[5,1280,3,192]{3,2,0,1:T(4,128)(2,1)}), bf16[5,1280,3,192]{3,2,0,1:T(4,128)(2,1)}, u32[]{:S(2)}, u32[]{:S(2)}) async-start(bf16[5,1280,3,192]{3,2,0,1:T(4,128)(2,1)} %copy.87), calls=%async_computation.3 | async-start | bytes 26214400 | tf_op jit(solution)/shard_map/all_to_all | solution.py:181
  972.1 212.1 %reduce-scatter.17.cloned.1.call-start = ((), (), s32[]{:S(2)}) async-start(), calls=%async_computation.13 | async-start | bytes 2654208 | tf_op jit(solution)/shard_map/reduce_scatter | solution.py:201
  978.5 321.3 %reduce-scatter.15.cloned.1.call-start = ((), (), s32[]{:S(2)}) async-start(), calls=%async_computation.12 | async-start | bytes 7962624 | tf_op jit(solution)/shard_map/reduce_scatter | solution.py:200
  1169.5 295.2 %reduce-scatter.23.cloned.1.call-start = ((), (), s32[]{:S(2)}) async-start(), calls=%async_computation.16 | async-start | bytes 10616832 | tf_op jit(solution)/shard_map/reduce_scatter | solution.py:203
  1184.1 2.1 copy-start.20
  1184.2 302.8 %reduce-scatter.27.cloned.1.call-start = ((), (), s32[]{:S(2)}) async-start(), calls=%async_computation.18 | async-start | bytes 491520
  1186.1 466.4 %reduce-scatter.19.cloned.1.call-start = ((), (), s32[]{:S(2)}) async-start(), calls=%async_computation.14 | async-start | bytes 10616832 | tf_op jit(solution)/shard_map/reduce_scatter | solution.py:202
  1202.3 265.1 %copy-start.9 = (f32[5,320]{1,0:T(8,128)S(1)}, f32[5,320]{1,0:T(8,128)}, u32[]{:S(2)}) copy-start(f32[5,320]{1,0:T(8,128)} %copy-done.8) | copy-start | bytes 19204
  1202.4 521.4 %reduce-scatter.25.cloned.1.call-start = ((), (), s32[]{:S(2)}) async-start(), calls=%async_computation.17 | async-start | bytes 1474560
  1302.4 423.1 %reduce-scatter.29.cloned.1.call-start = ((), (), s32[]{:S(2)}) async-start(), calls=%async_computation.19 | async-start | bytes 1474560
  1467.4 269.9 %reduce-scatter.21.cloned.1.call-start = ((), (), s32[]{:S(2)}) async-start(), calls=%async_computation.15 | async-start | bytes 1474560 | tf_op jit(solution)/shard_map/reduce_scatter | solution.py:208
  1470.4 182.2 %copy-start.14 = (f32[768]{0:T(1024)S(1)}, f32[768]{0:T(1024)}, u32[]{:S(2)}) copy-start(f32[768]{0:T(1024)} %copy-done.13) | copy-start | bytes 9220
  1470.4 182.2 %copy-start.16 = (f32[1600]{0:T(1024)S(1)}, f32[1600]{0:T(1024)}, u32[]{:S(2)}) copy-start(f32[1600]{0:T(1024)} %div.27) | copy-start | bytes 19204
  1652.6 14.2 copy-start.18
  1673.1 3.8 copy-start.23
  1673.1 9.3 copy-start.27
  (6 other events, 5.9 us)
Sparse Core Ops, SparseCore 0:
  978.7 71.9 reduce-scatter.16
  1169.6 130.1 reduce-scatter.14
  1303.4 161.2 reduce-scatter.22
  1467.0 19.8 reduce-scatter.26
  1490.4 162.0 reduce-scatter.18
  1654.9 24.7 reduce-scatter.24
  1682.8 25.6 reduce-scatter.28
  1711.6 25.5 reduce-scatter.20
where the time goes:
time: 1760 us; the launch traced here: 1740 us
  waiting for transfers between devices  780 us (44%)
  matrix products  436 us (25%)
  local copies, waits for them, and re-layouts  250 us (14%)
  other arithmetic  198 us (11%)
  blocking collectives  41.3 us (2%)
  starting transfers between devices  23.2 us (1%)
    reduce_scatter x1, waiting for transfers between devices, per_device(): lax.psum_scatter(grad_wup, 'dp', scatter_dimension=0, tiled=True)  164 us
    reduce_scatter x1, waiting for transfers between devices, per_device(): lax.psum_scatter(grad_wdown, 'dp', scatter_dimension=0, tiled=True)  162 us
    all_to_all x1, waiting for transfers between devices, per_device(): lax.all_to_all(grad_stacked, 'mix', split_axis=1, concat_axis=3, tiled=True)  137 us
    all_to_all x1, waiting for transfers between devices, per_device(): lax.all_to_all(joined.astype(jnp.bfloat16).reshape(item_dev, slot_dev, 3,...  130 us
    reduce_scatter x1, waiting for transfers between devices, per_device(): lax.psum_scatter(grad_wqkv, 'dp', scatter_dimension=0, tiled=True)  97.4 us
    dot_general x10, matrix products, score_table(): jnp.einsum('qhd,khd->hqk', queries, key_rows, preferred_element_type=jnp....  90 us
    convert_element_type x5, other arithmetic, attend_back(): grad_scores = (probs * (grad_probs - row_inner)).astype(jnp.bfloat16)  66.2 us
    dot_general x5, matrix products, attend_back(): jnp.einsum('qhd,khd->hqk', grad_part, value_rows, preferred_element_type=...  61.7 us
  transfers between devices with their start and end apart: 12, of which 9 were waited for; matrix products, arithmetic and copies ran while one was open for 9% of the time, Pallas kernels for 0%

commit v1 on v0

v1 whole, which is shorter than its diff:
```python
import functools
import math

import jax
import jax.numpy as jnp
from jax import lax
from jax.experimental import pallas as pl
from jax.experimental.pallas import tpu as pltpu
from jax.sharding import PartitionSpec as P

HEAD = 64
PASSES = 5
EPS = 1e-05
NEG = -1e30
BF = jnp.bfloat16
F32 = jnp.float32
VMEM_LIMIT = 62 * 1024 * 1024
TILE = 256


def dg(a, b, ca, cb):
    return lax.dot_general(a, b, (((ca,), (cb,)), ((), ())), preferred_element_type=F32)


def params(n=1, limit=VMEM_LIMIT):
    return pltpu.CompilerParams(
        dimension_semantics=("arbitrary",) * n, vmem_limit_bytes=limit
    )


def const_spec(shape):
    zeros = (0,) * len(shape)
    return pl.BlockSpec(shape, lambda *_: zeros, pipeline_mode=pl.Buffered(1))


def cost(flops, nbytes, trans=0):
    return pl.CostEstimate(flops=int(flops), bytes_accessed=int(nbytes), transcendentals=int(trans))


def ln_stats(values):
    center = values - jnp.mean(values, axis=-1, keepdims=True)
    inverse = lax.rsqrt(jnp.mean(center * center, axis=-1, keepdims=True) + EPS)
    return center * inverse, inverse


def ln_back(upstream, normed, inverse, gain):
    scaled = upstream * gain
    inner = scaled - jnp.mean(scaled, axis=-1, keepdims=True)
    inner = inner - normed * jnp.mean(scaled * normed, axis=-1, keepdims=True)
    return inverse * inner


def qkv_body(x_ref, pe_ref, g_ref, b_ref, w_ref, bias_ref, scale_ref, o_ref):
    hidden = x_ref[...].astype(F32) + pe_ref[...].astype(F32)
    normed, _ = ln_stats(hidden)
    low = (normed * g_ref[...] + b_ref[...]).astype(BF)
    out = dg(low, w_ref[...], 1, 0) + bias_ref[...]
    o_ref[...] = (out * scale_ref[...]).astype(BF)


def qkv_whole(x, pe, gain, bias, w, wb, ws):
    rows, width = x.shape
    tile = pe.shape[0]
    cols = w.shape[1]
    return pl.pallas_call(
        qkv_body,
        grid=(rows // tile,),
        in_specs=[
            pl.BlockSpec((tile, width), lambda i: (i, 0)),
            const_spec((tile, width)),
            const_spec((1, width)),
            const_spec((1, width)),
            const_spec((width, cols)),
            const_spec((1, cols)),
            const_spec((1, cols)),
        ],
        out_specs=pl.BlockSpec((tile, cols), lambda i: (i, 0)),
        out_shape=jax.ShapeDtypeStruct((rows, cols), BF),
        compiler_params=params(),
        cost_estimate=cost(2 * rows * width * cols, 2 * (rows * (width + cols) + width * cols)),
        name="qkv_whole",
    )(x, pe, gain, bias, w, wb, ws)


def qkv_split_body(x_ref, pe_ref, g_ref, b_ref, w_ref, bias_ref, scale_ref, o_ref):
    hidden = x_ref[...].astype(F32) + pe_ref[...].astype(F32)
    normed, _ = ln_stats(hidden)
    low = (normed * g_ref[...] + b_ref[...]).astype(BF)
    for part in range(w_ref.shape[0]):
        out = dg(low, w_ref[part], 1, 0) + bias_ref[part]
        o_ref[part] = (out * scale_ref[...]).astype(BF)


def qkv_split(x, pe, gain, bias, w, wb, ws):
    rows, width = x.shape
    parts, _, cols = w.shape
    return pl.pallas_call(
        qkv_split_body,
        out_shape=jax.ShapeDtypeStruct((parts, rows, cols), BF),
        compiler_params=pltpu.CompilerParams(vmem_limit_bytes=VMEM_LIMIT),
        cost_estimate=cost(2 * rows * width * cols * parts, 2 * parts * cols * (rows + width)),
        name="qkv_split",
    )(x, pe, gain, bias, w, wb, ws)


def head_mask(block, half):
    lane = lax.broadcasted_iota(jnp.int32, block.shape, 1)
    return jnp.where((lane // HEAD) == half, block, jnp.zeros_like(block))


def causal(scores):
    row = lax.broadcasted_iota(jnp.int32, scores.shape, 0)
    col = lax.broadcasted_iota(jnp.int32, scores.shape, 1)
    return jnp.where(row <= col, scores, NEG)


def score_tile(k, q_tile, kb, lo, hi):
    s = dg(k[:hi], q_tile, 1, 1)
    s = s + kb[:hi]
    if lo:
        return jnp.concatenate([s[:lo], causal(s[lo:])], axis=0)
    return causal(s)


def forward_heads(keys, queries, vt_ref, kb_ref, lse_ref, store):
    slots = keys[0].shape[0]
    count = len(queries)
    for lo in range(0, slots, TILE):
        hi = lo + TILE
        outs = []
        for h in range(count):
            s = score_tile(keys[h], queries[h][lo:hi], kb_ref, lo, hi)
            top = jnp.max(s, axis=0, keepdims=True)
            p = jnp.exp(s - top).astype(BF)
            o = dg(vt_ref[h, :, :hi], p, 1, 0)
            total = o[HEAD : HEAD + 1]
            outs.append(o[:HEAD] * (1.0 / total))
            lse_ref[h : h + 1, lo:hi] = top + jnp.log(total)
        store(lo, hi, jnp.concatenate(outs, axis=0).T.astype(BF))


def fill_vt(vt_ref, value_block, count):
    vt = value_block.T
    for h in range(count):
        vt_ref[h, :HEAD, :] = vt[h * HEAD : (h + 1) * HEAD]
        vt_ref[h, HEAD:, :] = jnp.ones((16, vt.shape[1]), BF)


def attend_whole_body(q_ref, k_ref, v_ref, kb_ref, o_ref, lse_ref, vt_ref):
    q = q_ref[...]
    k = k_ref[...]
    fill_vt(vt_ref, v_ref[...], 2)

    def store(lo, hi, value):
        o_ref[lo:hi, :] = value

    forward_heads([k, k], [head_mask(q, 0), head_mask(q, 1)], vt_ref, kb_ref, lse_ref.at[0], store)


def attend_whole(qkv, kb):
    slots, cols = qkv.shape
    width = cols // 3
    pairs = width // (2 * HEAD)
    block = lambda off: pl.BlockSpec((slots, 2 * HEAD), lambda j: (0, off * pairs + j))
    area = slots * slots * 0.6
    return pl.pallas_call(
        attend_whole_body,
        grid=(pairs,),
        in_specs=[block(0), block(1), block(2), const_spec(kb.shape)],
        out_specs=[block(0), pl.BlockSpec((1, 8, slots), lambda j: (j, 0, 0))],
        out_shape=[
            jax.ShapeDtypeStruct((slots, width), BF),
            jax.ShapeDtypeStruct((pairs, 8, slots), F32),
        ],
        scratch_shapes=[pltpu.VMEM((2, HEAD + 16, slots), BF)],
        compiler_params=params(),
        cost_estimate=cost(8 * area * width * 4, 8 * slots * width, area * pairs * 2),
        name="attend_whole",
    )(qkv, qkv, qkv, kb)


def cut(block, part, h, count):
    base = (part * count + h) * HEAD
    return block[:, base : base + HEAD]


def attend_split_body(qkv_ref, kb_ref, o_ref, lse_ref, vt_ref):
    block = qkv_ref[...]
    count = block.shape[1] // (3 * HEAD)
    fill_vt(vt_ref, block[:, 2 * count * HEAD :], count)

    def store(lo, hi, value):
        o_ref[lo:hi, :] = value

    keys = [cut(block, 1, h, count) for h in range(count)]
    queries = [cut(block, 0, h, count) for h in range(count)]
    forward_heads(keys, queries, vt_ref, kb_ref, lse_ref, store)


def attend_split(qkv, kb):
    slots, cols = qkv.shape
    count = cols // (3 * HEAD)
    area = slots * slots * 0.6
    return pl.pallas_call(
        attend_split_body,
        out_shape=[
            jax.ShapeDtypeStruct((slots, count * HEAD), BF),
            jax.ShapeDtypeStruct((8, slots), F32),
        ],
        scratch_shapes=[pltpu.VMEM((count, HEAD + 16, slots), BF)],
        compiler_params=pltpu.CompilerParams(vmem_limit_bytes=VMEM_LIMIT),
        cost_estimate=cost(8 * area * count * HEAD * 4, 8 * slots * cols, area * count),
        name="attend_split",
    )(qkv, kb)


def inner_rows(d_ref, do, o, count):
    prod = (do.astype(F32) * o.astype(F32)).T
    for h in range(count):
        d_ref[h : h + 1, :] = jnp.sum(prod[h * HEAD : (h + 1) * HEAD], axis=0, keepdims=True)


def backward_tile(k, v, kt, q_tile, do_tile, kb_ref, lse_row, d_row, lo, hi):
    s = score_tile(k, q_tile, kb_ref, lo, hi)
    p = jnp.exp(s - lse_row)
    dp = dg(v[:hi], do_tile, 1, 1)
    ds = (p * (dp - d_row)).astype(BF)
    dqt = dg(kt[:, :hi], ds, 1, 0)
    return p.astype(BF), ds, dqt


def back_whole_body(q_ref, k_ref, v_ref, do_ref, o_ref, lse_ref, kb_ref, out_ref, d_ref, kt_ref, dk_ref, dv_ref):
    q, k, v, do = q_ref[...], k_ref[...], v_ref[...], do_ref[...]
    slots = q.shape[0]
    inner_rows(d_ref, do, o_ref[...], 2)
    kt_ref[...] = k.T
    queries = [head_mask(q, h) for h in range(2)]
    grads = [head_mask(do, h) for h in range(2)]
    for lo in reversed(range(0, slots, TILE)):
        hi = lo + TILE
        got = [
            backward_tile(
                k,
                v,
                kt_ref[h * HEAD : (h + 1) * HEAD, :],
                queries[h][lo:hi],
                grads[h][lo:hi],
                kb_ref,
                lse_ref[0, h : h + 1, lo:hi],
                d_ref[h : h + 1, lo:hi],
                lo,
                hi,
            )
            for h in range(2)
        ]
        dv = dg(
            jnp.concatenate([got[0][0], got[1][0]], axis=1),
            jnp.concatenate([grads[0][lo:hi], grads[1][lo:hi]], axis=0),
            1,
            0,
        )
        dk = dg(
            jnp.concatenate([got[0][1], got[1][1]], axis=1),
            jnp.concatenate([queries[0][lo:hi], queries[1][lo:hi]], axis=0),
            1,
            0,
        )
        if hi == slots:
            dv_ref[...] = dv
            dk_ref[...] = dk
        else:
            dv_ref[:hi, :] += dv
            dk_ref[:hi, :] += dk
        dqt = jnp.concatenate([got[0][2], got[1][2]], axis=0)
        out_ref[0, lo:hi, :] = (dqt.T * (1.0 / math.sqrt(HEAD))).astype(BF)
    out_ref[1] = dk_ref[...].astype(BF)
    out_ref[2] = dv_ref[...].astype(BF)


def back_whole(qkv, do, att, lse, kb):
    slots, cols = qkv.shape
    width = cols // 3
    pairs = width // (2 * HEAD)
    block = lambda off: pl.BlockSpec((slots, 2 * HEAD), lambda j: (0, off * pairs + j))
    area = slots * slots * 0.6
    return pl.pallas_call(
        back_whole_body,
        grid=(pairs,),
        in_specs=[
            block(0),
            block(1),
            block(2),
            block(0),
            block(0),
            pl.BlockSpec((1, 8, slots), lambda j: (j, 0, 0)),
            const_spec(kb.shape),
        ],
        out_specs=pl.BlockSpec((3, slots, 2 * HEAD), lambda j: (0, 0, j)),
        out_shape=jax.ShapeDtypeStruct((3, slots, width), BF),
        scratch_shapes=[
            pltpu.VMEM((8, slots), F32),
            pltpu.VMEM((2 * HEAD, slots), BF),
            pltpu.VMEM((slots, 2 * HEAD), F32),
            pltpu.VMEM((slots, 2 * HEAD), F32),
        ],
        compiler_params=params(),
        cost_estimate=cost(20 * area * width * 4, 16 * slots * width, area * pairs * 2),
        name="back_whole",
    )(qkv, qkv, qkv, do, att, lse, kb)


def back_split_body(qkv_ref, do_ref, o_ref, lse_ref, kb_ref, out_ref, d_ref, kt_ref, dk_ref, dv_ref):
    block, do = qkv_ref[...], do_ref[...]
    slots = block.shape[0]
    count = block.shape[1] // (3 * HEAD)
    wide = count * HEAD
    inner_rows(d_ref, do, o_ref[...], count)
    kt_ref[...] = block[:, wide : 2 * wide].T
    queries = [cut(block, 0, h, count) for h in range(count)]
    keys = [cut(block, 1, h, count) for h in range(count)]
    values = [cut(block, 2, h, count) for h in range(count)]
    grads = [do[:, h * HEAD : (h + 1) * HEAD] for h in range(count)]
    for lo in reversed(range(0, slots, TILE)):
        hi = lo + TILE
        dqts = []
        for h in range(count):
            p, ds, dqt = backward_tile(
                keys[h],
                values[h],
                kt_ref[h * HEAD : (h + 1) * HEAD, :],
                queries[h][lo:hi],
                grads[h][lo:hi],
                kb_ref,
                lse_ref[h : h + 1, lo:hi],
                d_ref[h : h + 1, lo:hi],
                lo,
                hi,
            )
            dqts.append(dqt)
            dv = dg(p, grads[h][lo:hi], 1, 0)
            dk = dg(ds, queries[h][lo:hi], 1, 0)
            if hi == slots:
                dv_ref[h] = dv
                dk_ref[h] = dk
            else:
                dv_ref[h, :hi, :] += dv
                dk_ref[h, :hi, :] += dk
        dqt = jnp.concatenate(dqts, axis=0)
        out_ref[lo:hi, :wide] = (dqt.T * (1.0 / math.sqrt(HEAD))).astype(BF)
    for h in range(count):
        out_ref[:, wide + h * HEAD : wide + (h + 1) * HEAD] = dk_ref[h].astype(BF)
        out_ref[:, 2 * wide + h * HEAD : 2 * wide + (h + 1) * HEAD] = dv_ref[h].astype(BF)


def back_split(qkv, do, att, lse, kb):
    slots, cols = qkv.shape
    count = cols // (3 * HEAD)
    area = slots * slots * 0.6
    return pl.pallas_call(
        back_split_body,
        out_shape=jax.ShapeDtypeStruct((slots, cols), BF),
        scratch_shapes=[
            pltpu.VMEM((8, slots), F32),
            pltpu.VMEM((count * HEAD, slots), BF),
            pltpu.VMEM((count, slots, HEAD), F32),
            pltpu.VMEM((count, slots, HEAD), F32),
        ],
        compiler_params=pltpu.CompilerParams(vmem_limit_bytes=VMEM_LIMIT),
        cost_estimate=cost(20 * area * count * HEAD * 4, 8 * slots * cols, area * count),
        name="back_split",
    )(qkv, do, att, lse, kb)


def mlp_body(
    xm_ref,
    x4_ref,
    cm_ref,
    c4_ref,
    am_ref,
    a4_ref,
    pe_ref,
    keep_ref,
    wo_ref,
    bo_ref,
    g2_ref,
    b2_ref,
    bd_ref,
    wu_ref,
    bu_ref,
    wd_ref,
    outm_ref,
    out4_ref,
    gmm_ref,
    gm4_ref,
    dam_ref,
    da4_ref,
    gwu_ref,
    gwd_ref,
    gwo_ref,
    gbu_ref,
    small_ref,
    mixed_ref,
    acc_ref,
    gsl_ref,
    sl_ref,
    gm_ref,
    slt_ref,
    gmt_ref,
    att_ref,
    gbd_ref,
    act_ref,
    gp_ref,
):
    step = pl.program_id(0)
    last = pl.num_programs(0) - 1
    tile = pe_ref.shape[0]
    rows = mixed_ref.shape[0]
    whole_tiles = xm_ref.shape[0] // tile
    parts = a4_ref.shape[0]
    piece = a4_ref.shape[2]

    def prologue(row, x, cot, keep, att):
        hidden = x.astype(F32) + pe_ref[...].astype(F32)
        mixed = hidden + keep * (dg(att, wo_ref[...], 1, 0) + bo_ref[...])
        mixed_ref[pl.ds(row, tile), :] = mixed
        normed, _ = ln_stats(mixed)
        sl_ref[pl.ds(row, tile), :] = (normed * g2_ref[...] + b2_ref[...]).astype(BF)
        gm = keep * cot.astype(F32)
        gm_ref[pl.ds(row, tile), :] = gm.astype(BF)
        gbd_ref[...] += jnp.sum(gm, axis=0, keepdims=True)

    @pl.when(step == 0)
    def _():
        gbd_ref[...] = jnp.zeros_like(gbd_ref)
        for part in range(parts):
            att_ref[:, part * piece : (part + 1) * piece] = a4_ref[part]

        def loop(i, carry):
            row = pl.multiple_of(i * tile, tile)
            prologue(
                row,
                xm_ref[pl.ds(row, tile), :],
                cm_ref[pl.ds(row, tile), :],
                keep_ref[:, 0:1],
                am_ref[pl.ds(row, tile), :],
            )
            return carry

        lax.fori_loop(0, whole_tiles, loop, 0)
        prologue(whole_tiles * tile, x4_ref[...], c4_ref[...], keep_ref[:, 1:2], att_ref[...])
        slt_ref[...] = sl_ref[...].T
        gmt_ref[...] = gm_ref[...].T

    @pl.when(step == 0)
    def _():
        acc_ref[...] = jnp.zeros_like(acc_ref)
        gsl_ref[...] = jnp.zeros_like(gsl_ref)

    root = math.sqrt(2.0 / math.pi)
    bias_sum = jnp.zeros(bu_ref.shape, F32)
    half_rows = rows // 2
    for part in range(2):
        span = pl.ds(part * half_rows, half_rows)
        pre = dg(sl_ref[span, :], wu_ref[...], 1, 0) + bu_ref[...]
        square = pre * pre
        tanh = jnp.tanh(root * pre * (1.0 + 0.044715 * square))
        half = 0.5 * (1.0 + tanh)
        act = (pre * half).astype(BF)
        act_ref[span, :] = act
        slope = half + 0.5 * pre * (1.0 - tanh * tanh) * (
            root * (1.0 + (3.0 * 0.044715) * square)
        )
        grad_pre = (dg(gm_ref[span, :], wd_ref[...], 1, 1) * slope).astype(BF)
        gp_ref[span, :] = grad_pre
        bias_sum += jnp.sum(grad_pre.astype(F32), axis=0, keepdims=True)
        acc_ref[span, :] += dg(act, wd_ref[...], 1, 0)
        gsl_ref[span, :] += dg(grad_pre, wu_ref[...], 1, 1)
    gbu_ref[0] = bias_sum

    gwd = dg(gmt_ref[...], act_ref[...], 1, 0).astype(BF)
    shard = gwd_ref.shape[2]
    for part in range(gwd_ref.shape[0]):
        gwd_ref[part, 0] = gwd[part * shard : (part + 1) * shard]
    gwu_ref[0] = dg(slt_ref[...], gp_ref[...], 1, 0).astype(BF)

    def epilogue(row, cot, keep):
        mixed = mixed_ref[pl.ds(row, tile), :]
        out = mixed + keep * (acc_ref[pl.ds(row, tile), :] + bd_ref[...])
        normed, inverse = ln_stats(mixed)
        up = gsl_ref[pl.ds(row, tile), :]
        small_ref[1:2, :] += jnp.sum(up * normed, axis=0, keepdims=True)
        small_ref[2:3, :] += jnp.sum(up, axis=0, keepdims=True)
        grad_mixed = cot.astype(F32) + ln_back(up, normed, inverse, g2_ref[...])
        grad_attn = (keep * grad_mixed).astype(BF)
        gm_ref[pl.ds(row, tile), :] = grad_attn
        small_ref[3:4, :] += jnp.sum(grad_attn.astype(F32), axis=0, keepdims=True)
        return out, grad_mixed.astype(BF), dg(grad_attn, wo_ref[...], 1, 1).astype(BF)

    @pl.when(step == last)
    def _():
        small_ref[...] = jnp.zeros_like(small_ref)
        small_ref[0:1, :] = gbd_ref[...]

        def loop(i, carry):
            row = pl.multiple_of(i * tile, tile)
            out, grad_mixed, grad_att = epilogue(row, cm_ref[pl.ds(row, tile), :], keep_ref[:, 0:1])
            outm_ref[pl.ds(row, tile), :] = out.astype(BF)
            gmm_ref[pl.ds(row, tile), :] = grad_mixed
            dam_ref[pl.ds(row, tile), :] = grad_att
            return carry

        lax.fori_loop(0, whole_tiles, loop, 0)
        base = whole_tiles * tile
        out, grad_mixed, grad_att = epilogue(base, c4_ref[...], keep_ref[:, 1:2])
        out4_ref[...] = out
        gm4_ref[...] = grad_mixed
        for part in range(parts):
            da4_ref[part] = grad_att[:, part * piece : (part + 1) * piece]
        slt_ref[:, :base] = am_ref[...].T
        slt_ref[:, base:] = att_ref[...].T
        gwo = dg(slt_ref[...], gm_ref[...], 1, 0).astype(BF)
        for part in range(parts):
            gwo_ref[part] = gwo[:, part * piece : (part + 1) * piece]


def mlp(xm, x4, cm, c4, am, a4, pe, keep, wo, bo, g2, b2, bd, wu, bu, wd, dp):
    rows_m, width = xm.shape
    rows_4 = x4.shape[0]
    rows = rows_m + rows_4
    wide = wu.shape[1]
    parts = a4.shape[0]
    piece = a4.shape[2]
    chunk = 384
    steps = wide // chunk
    block_cols = wide // parts
    per = block_cols // chunk
    out_shape = [
        jax.ShapeDtypeStruct((rows_m, width), BF),
        jax.ShapeDtypeStruct((rows_4, width), F32),
        jax.ShapeDtypeStruct((rows_m, width), BF),
        jax.ShapeDtypeStruct((rows_4, width), BF),
        jax.ShapeDtypeStruct((rows_m, width), BF),
        jax.ShapeDtypeStruct((parts, rows_4, piece), BF),
        jax.ShapeDtypeStruct((parts, width, block_cols), BF),
        jax.ShapeDtypeStruct((parts, steps, width // parts, chunk), BF),
        jax.ShapeDtypeStruct((parts, width, piece), BF),
        jax.ShapeDtypeStruct((steps, 1, chunk), F32),
        jax.ShapeDtypeStruct((8, width), F32),
    ]
    ins = [xm, x4, cm, c4, am, a4, pe, keep, wo, bo, g2, b2, bd]
    in_specs = [const_spec(a.shape) for a in ins] + [
        pl.BlockSpec((width, chunk), lambda c: (0, c)),
        pl.BlockSpec((1, chunk), lambda c: (0, c)),
        pl.BlockSpec((chunk, width), lambda c: (c, 0)),
    ]
    out_specs = [const_spec(s.shape) for s in out_shape[:6]] + [
        pl.BlockSpec((1, width, chunk), lambda c: (c // per, 0, c % per)),
        pl.BlockSpec((parts, 1, width // parts, chunk), lambda c: (0, c, 0, 0)),
        const_spec(out_shape[8].shape),
        pl.BlockSpec((1, 1, chunk), lambda c: (c, 0, 0)),
        const_spec(out_shape[10].shape),
    ]
    return pl.pallas_call(
        mlp_body,
        grid=(steps,),
        in_specs=in_specs,
        out_specs=out_specs,
        out_shape=out_shape,
        scratch_shapes=[
            pltpu.VMEM((rows, width), F32),
            pltpu.VMEM((rows, width), F32),
            pltpu.VMEM((rows, width), F32),
            pltpu.VMEM((rows, width), BF),
            pltpu.VMEM((rows, width), BF),
            pltpu.VMEM((width, rows), BF),
            pltpu.VMEM((width, rows), BF),
            pltpu.VMEM((rows_4, width), BF),
            pltpu.VMEM((1, width), F32),
            pltpu.VMEM((rows, chunk), BF),
            pltpu.VMEM((rows, chunk), BF),
        ],
        compiler_params=params(),
        cost_estimate=cost(
            12 * rows * width * wide + 6 * rows * width * width, 16 * rows * width, rows * wide
        ),
        name="mlp",
    )(*ins, wu, bu, wd)


def assemble(d4_ref, src_ref):
    parts, _, cols = src_ref.shape
    piece = cols // 3
    width = parts * piece
    for kind in range(3):
        for part in range(parts):
            d4_ref[:, kind * width + part * piece : kind * width + (part + 1) * piece] = src_ref[
                part, :, kind * piece : (kind + 1) * piece
            ]


def wqkv_body(xm_ref, x4_ref, pe_ref, g_ref, b_ref, dm_ref, d4_ref, gw_ref, sums_ref, low_ref, flat_ref, cur_ref):
    tile = pe_ref.shape[0]
    whole_tiles = xm_ref.shape[0] // tile
    base = whole_tiles * tile
    width = xm_ref.shape[1]
    parts = gw_ref.shape[0]
    cols = gw_ref.shape[2]
    rows4, wide = flat_ref.shape

    def first(row, x):
        normed, _ = ln_stats(x.astype(F32) + pe_ref[...].astype(F32))
        low_ref[pl.ds(row, tile), :] = (normed * g_ref[...] + b_ref[...]).astype(BF)

    def loop(i, carry):
        row = pl.multiple_of(i * tile, tile)
        first(row, xm_ref[pl.ds(row, tile), :])
        return carry

    lax.fori_loop(0, whole_tiles, loop, 0)
    first(base, x4_ref[...])
    low_t = low_ref[...].T
    assemble(flat_ref, d4_ref)
    chunk = 256
    for c in range(wide // chunk):
        off = c * chunk
        kind, inner = off // width, off % width
        cur_ref[:base, :] = dm_ref[kind, :, inner : inner + chunk]
        cur_ref[base:, :] = flat_ref[:, off : off + chunk]
        cur = cur_ref[...]
        sums_ref[:, off : off + chunk] = jnp.sum(cur.astype(F32), axis=0, keepdims=True)
        got = dg(low_t, cur, 1, 0).astype(BF)
        at = off
        while at < off + chunk:
            part = at // cols
            end = min(off + chunk, (part + 1) * cols)
            gw_ref[part, :, at - part * cols : end - part * cols] = got[:, at - off : end - off]
            at = end


def wqkv_grad(xm, x4, pe, gain, bias, dm, d4):
    rows_m, width = xm.shape
    rows_4 = x4.shape[0]
    rows = rows_m + rows_4
    parts = d4.shape[0]
    wide = 3 * width
    return pl.pallas_call(
        wqkv_body,
        out_shape=[
            jax.ShapeDtypeStruct((parts, width, wide // parts), BF),
            jax.ShapeDtypeStruct((1, wide), F32),
        ],
        scratch_shapes=[
            pltpu.VMEM((rows, width), BF),
            pltpu.VMEM((rows_4, wide), BF),
            pltpu.VMEM((rows, 256), BF),
        ],
        compiler_params=pltpu.CompilerParams(vmem_limit_bytes=VMEM_LIMIT),
        cost_estimate=cost(2 * rows * width * wide, 2 * (rows * (width + wide) + width * wide)),
        name="wqkv_grad",
    )(xm, x4, pe, gain, bias, dm, d4)


def input_body(xm_ref, x4_ref, pe_ref, g_ref, w_ref, hot_ref, gmm_ref, gm4_ref, dm_ref, d4_ref, gxm_ref, gx4_ref, small_ref, flat_ref):
    tile = pe_ref.shape[0]
    whole_tiles = xm_ref.shape[0] // tile
    base = whole_tiles * tile
    width = xm_ref.shape[1]
    small_ref[...] = jnp.zeros_like(small_ref)
    assemble(flat_ref, d4_ref)

    def finish(x, grad_mixed, up):
        normed, inverse = ln_stats(x.astype(F32) + pe_ref[...].astype(F32))
        small_ref[8:9, :] += jnp.sum(up * normed, axis=0, keepdims=True)
        small_ref[9:10, :] += jnp.sum(up, axis=0, keepdims=True)
        grad = grad_mixed.astype(F32) + ln_back(up, normed, inverse, g_ref[...])
        high = grad.astype(BF)
        rest = (grad - high.astype(F32)).astype(BF)
        small_ref[0:8, :] += dg(hot_ref[...], high, 1, 0) + dg(hot_ref[...], rest, 1, 0)
        return grad

    def loop(i, carry):
        row = pl.multiple_of(i * tile, tile)
        up = dg(dm_ref[0, pl.ds(row, tile), :], w_ref[:, :width], 1, 1)
        up += dg(dm_ref[1, pl.ds(row, tile), :], w_ref[:, width : 2 * width], 1, 1)
        up += dg(dm_ref[2, pl.ds(row, tile), :], w_ref[:, 2 * width :], 1, 1)
        gxm_ref[pl.ds(row, tile), :] = finish(
            xm_ref[pl.ds(row, tile), :], gmm_ref[pl.ds(row, tile), :], up
        ).astype(BF)
        return carry

    lax.fori_loop(0, whole_tiles, loop, 0)
    gx4_ref[...] = finish(x4_ref[...], gm4_ref[...], dg(flat_ref[...], w_ref[...], 1, 1))


def input_grad(xm, x4, pe, gain, w, hot, gmm, gm4, dm, d4):
    rows_m, width = xm.shape
    rows_4 = x4.shape[0]
    rows = rows_m + rows_4
    wide = w.shape[1]
    return pl.pallas_call(
        input_body,
        out_shape=[
            jax.ShapeDtypeStruct((rows_m, width), BF),
            jax.ShapeDtypeStruct((rows_4, width), F32),
            jax.ShapeDtypeStruct((16, width), F32),
        ],
        scratch_shapes=[pltpu.VMEM((rows_4, wide), BF)],
        compiler_params=pltpu.CompilerParams(vmem_limit_bytes=VMEM_LIMIT),
        cost_estimate=cost(2 * rows * width * wide, 2 * (rows * (width + wide) + width * wide)),
        name="input_grad",
    )(xm, x4, pe, gain, w, hot, gmm, gm4, dm, d4)


def swap(value, axis, size, bit):
    return lax.ppermute(value, axis, [(i, i ^ bit) for i in range(size)])


def halve(value, dim, axis, size, bit, last=False):
    mine = (lax.axis_index(axis) // bit) % 2
    keep = lax.dynamic_index_in_dim(value, mine, dim, keepdims=False)
    send = lax.dynamic_index_in_dim(value, 1 - mine, dim, keepdims=False)
    got = swap(send, axis, size, bit)
    total = keep.astype(F32) + got.astype(F32)
    return total if last else total.astype(BF)


def reduce_shard(grad, dp, mix, order):
    _, _, r, c = grad.shape
    if mix != 4 or dp != 8:
        total = lax.psum_scatter(grad, "mix", scatter_dimension=0, tiled=False)
        return lax.psum_scatter(total, "dp", scatter_dimension=0, tiled=False).astype(F32)
    value = grad.reshape(2, 2, 2, 2, 2, r, c)
    names = ["y", "core", "z1", "z0", "x"]
    spots = {"y": ("mix", 4, 2), "core": ("mix", 4, 1), "z1": ("dp", 8, 4), "z0": ("dp", 8, 2), "x": ("dp", 8, 1)}
    for index, name in enumerate(order):
        dim = names.index(name)
        names.pop(dim)
        value = halve(value, dim, *spots[name], last=index == len(order) - 1)
    return value


def sum_all(value, dp, mix):
    for axis, size in (("mix", mix), ("dp", dp)):
        bit = 1
        while bit < size:
            value = value + swap(value, axis, size, bit)
            bit *= 2
    return value


def per_device(
    mix,
    dp,
    inputs,
    pass_count,
    pass_embed,
    ln1_gain,
    ln1_bias,
    w_qkv,
    bias_q,
    bias_v,
    w_out,
    bias_out,
    ln2_gain,
    ln2_bias,
    w_up,
    bias_up,
    w_down,
    bias_down,
    cotangent,
):
    items, slot_dev, width = inputs.shape
    slots = slot_dev * mix
    place = lax.axis_index("mix")
    row = lambda v: v.astype(F32).reshape(1, -1)
    gain1, shift1, gain2, shift2 = row(ln1_gain), row(ln1_bias), row(ln2_gain), row(ln2_bias)

    pass_ids = lax.iota(jnp.int32, slot_dev) % PASSES
    hot = (lax.iota(jnp.int32, 8)[:, None] == pass_ids[None, :]).astype(BF)
    pe = jnp.dot(hot[:PASSES].T, pass_embed, preferred_element_type=F32).astype(BF)
    mine = lax.dynamic_index_in_dim(pass_count, place, keepdims=False)
    other = pass_count[items - 1]
    keep = jnp.stack([pass_ids < mine, pass_ids < other], axis=1).astype(F32)
    slot_pass = lax.iota(jnp.int32, slots) % PASSES
    bias_of = lambda n: jnp.broadcast_to(
        jnp.where(slot_pass < n, 0.0, NEG).astype(F32)[:, None], (slots, TILE)
    )
    kb_m, kb_4 = bias_of(mine), bias_of(other)

    scale = 1.0 / math.sqrt(HEAD)
    joined_bias = jnp.concatenate([row(bias_q), jnp.zeros((1, width), F32), row(bias_v)], axis=1)
    joined_scale = jnp.concatenate(
        [jnp.full((1, width), scale, F32), jnp.ones((1, 2 * width), F32)], axis=1
    )
    piece = width // mix
    regroup = lambda a: a.reshape(-1, 3, mix, piece).transpose(2, 0, 1, 3).reshape(mix, -1, 3 * piece)
    w_split = regroup(w_qkv)
    bias_split = regroup(joined_bias)
    scale_split = jnp.concatenate(
        [jnp.full((1, piece), scale, F32), jnp.ones((1, 2 * piece), F32)], axis=1
    )

    spread = lambda a: lax.all_to_all(a, "mix", 0, 0, tiled=False)

    xm = spread(inputs[: items - 1]).reshape(slots, width)
    cm = spread(cotangent[: items - 1]).reshape(slots, width)
    x4, c4 = inputs[items - 1], cotangent[items - 1]

    qkv4 = spread(qkv_split(x4, pe, gain1, shift1, w_split, bias_split, scale_split))
    qkv4 = qkv4.reshape(slots, 3 * piece)
    qkvm = qkv_whole(xm, pe, gain1, shift1, w_qkv, joined_bias, joined_scale)
    att4h, lse4 = attend_split(qkv4, kb_4)
    att4 = spread(att4h.reshape(mix, slot_dev, piece))
    attm, lsem = attend_whole(qkvm, kb_m)

    outm, out4, gmm, gm4, dam, da4, gwu, gwd, gwo, gbu, small2 = mlp(
        xm,
        x4,
        cm,
        c4,
        attm,
        att4,
        pe,
        keep,
        w_out,
        row(bias_out),
        gain2,
        shift2,
        row(bias_down),
        w_up,
        row(bias_up),
        w_down,
        dp,
    )
    da4h = spread(da4).reshape(slots, piece)
    out_rows = spread(outm.reshape(mix, slot_dev, width))
    wide = w_up.shape[1]
    gwu = gwu.reshape(mix, dp, width // dp, wide // mix)
    if dp == 8:
        pass
    else:
        gwd = gwd.transpose(0, 2, 1, 3).reshape(mix, width // mix, dp, wide // dp).transpose(0, 2, 1, 3)
    gwo = gwo.reshape(mix, dp, width // dp, piece)
    shard_up = reduce_shard(gwu, dp, mix, ["core", "x", "z1", "z0", "y"])
    shard_down = reduce_shard(gwd, dp, mix, ["core", "z1", "z0", "x", "y"]).T
    shard_out = reduce_shard(gwo, dp, mix, ["core", "x", "z1", "z0", "y"])
    small2, gbu = lax.psum((small2, gbu), ("dp", "mix"))

    dm = back_whole(qkvm, dam, attm, lsem, kb_m)
    d4 = back_split(qkv4, da4h, att4h, lse4, kb_4)
    d4 = spread(d4.reshape(mix, slot_dev, 3 * piece))
    gwq, sums = wqkv_grad(xm, x4, pe, gain1, shift1, dm, d4)
    shard_qkv = reduce_shard(
        gwq.reshape(mix, dp, width // dp, 3 * piece), dp, mix, ["core", "x", "z1", "z0", "y"]
    )
    gxm, gx4, small1 = input_grad(xm, x4, pe, gain1, w_qkv, hot, gmm, gm4, dm, d4)
    gx_rows = spread(gxm.reshape(mix, slot_dev, width))
    small1 = sum_all(
        jnp.concatenate([small1[:PASSES], small1[8:10], sums.reshape(3, width)], axis=0), dp, mix
    )

    result = jnp.concatenate([out_rows.astype(F32), out4[None]], axis=0)
    grad_x = jnp.concatenate([gx_rows.astype(F32), gx4[None]], axis=0)
    return (
        result,
        grad_x,
        small1[:PASSES],
        small1[PASSES],
        small1[PASSES + 1],
        shard_qkv,
        small1[PASSES + 2],
        small1[PASSES + 4],
        shard_out,
        small2[3],
        small2[1],
        small2[2],
        shard_up,
        gbu.reshape(-1),
        shard_down,
        small2[0],
    )


def solution(mesh):
    data = P("dp", "mix", None)
    none = P()
    return jax.shard_map(
        functools.partial(per_device, mesh.shape["mix"], mesh.shape["dp"]),
        mesh=mesh,
        in_specs=(data, P("dp")) + (none,) * 14 + (data,),
        out_specs=(
            data,
            data,
            none,
            none,
            none,
            P("dp", "mix"),
            none,
            none,
            P("dp", "mix"),
            none,
            none,
            none,
            P("dp", "mix"),
            none,
            P("dp", "mix"),
            none,
        ),
        check_vma=False,
    )
```

time: 1760 us -> 555 us (0.32)
  waiting for transfers between devices: 780 us -> 108 us
  matrix products: 436 us -> 1.16 us
  Pallas kernels: 0 us -> 240 us
  local copies, waits for them, and re-layouts: 250 us -> 60.2 us
  other arithmetic: 198 us -> 29.7 us
  starting transfers between devices: 23.2 us -> 64.7 us
    reduce_scatter x5 -> x0, waiting for transfers between devices: 435 us -> none  [the longest x1 164 us: per_device(): lax.psum_scatter(grad_wup, 'dp', scatter_dimension=0, tiled=True)]
    dot_general x49 -> x1, matrix products: 436 us -> 1.16 us  [per_device(): jnp.dot(hot[:PASSES].T, pass_embed, preferred_element_type=F32).astype(BF)]
    all_to_all x4 -> x8, waiting for transfers between devices: 343 us -> 28.9 us  [per_device(): spread = lambda a: lax.all_to_all(a, 'mix', 0, 0, tiled=False)]
    pallas_call x0 -> x9, Pallas kernels: none -> 240 us  [the longest x1 94.6 us: mlp(): pl.pallas_call(mlp_body, grid=(steps,), in_specs=in_specs, out_specs=out_...]
    all_to_all x7 -> x2, local copies, waits for them, and re-layouts: 82.8 us -> 2.29 us  [per_device(): spread = lambda a: lax.all_to_all(a, 'mix', 0, 0, tiled=False)]
    ppermute x0 -> x25, waiting for transfers between devices: none -> 79.1 us  [swap(): return lax.ppermute(value, axis, [(i, i ^ bit) for i in range(size)])]
    reduce_sum x12 -> x0, other arithmetic: 69.4 us -> none  [the longest x5 48.8 us: attend_item(): jnp.sum(jnp.exp(scores - row_max), axis=-1, keepdims=True)]
    convert_element_type x17 -> x20, other arithmetic: 85.3 us -> 16.8 us  [the longest x16 13.8 us: halve(): return total if last else total.astype(BF)]
  transfers between devices with their start and end apart: 12 -> 33, of which waited for: 9 -> 11; matrix products, arithmetic and copies ran while one was open for 9% -> 12% of each run, Pallas kernels for 0% -> 26%
where the time goes in v1:
time: 555 us; the launch traced here: 545 us
  Pallas kernels  240 us (43%)
  waiting for transfers between devices  108 us (19%)
  starting transfers between devices  64.7 us (12%)
  local copies, waits for them, and re-layouts  60.2 us (11%)
  blocking collectives  39.6 us (7%)
  other arithmetic  29.7 us (5%)
    pallas_call x1, Pallas kernels, mlp(): pl.pallas_call(mlp_body, grid=(steps,), in_specs=in_specs, out_specs=out_...  94.6 us
    ppermute x25, waiting for transfers between devices, swap(): return lax.ppermute(value, axis, [(i, i ^ bit) for i in range(size)])  79.1 us
    psum x1, blocking collectives, per_device(): small2, gbu = lax.psum((small2, gbu), ('dp', 'mix'))  39.6 us
    pallas_call x1, Pallas kernels, back_whole(): pl.pallas_call(back_whole_body, grid=(pairs,), in_specs=[block(0), block(...  39.6 us
    pallas_call x1, Pallas kernels, attend_whole(): pl.pallas_call(attend_whole_body, grid=(pairs,), in_specs=[block(0), bloc...  34.3 us
    all_to_all x8, starting transfers between devices, per_device(): spread = lambda a: lax.all_to_all(a, 'mix', 0, 0, tiled=False)  33.2 us
    ppermute x25, starting transfers between devices, swap(): return lax.ppermute(value, axis, [(i, i ^ bit) for i in range(size)])  31.5 us
    all_to_all x8, waiting for transfers between devices, per_device(): spread = lambda a: lax.all_to_all(a, 'mix', 0, 0, tiled=False)  28.9 us
  transfers between devices with their start and end apart: 33, of which 11 were waited for; matrix products, arithmetic and copies ran while one was open for 12% of the time, Pallas kernels for 26%

profile of v1, /device:TPU:0, one launch (start us, length us, event | category | flops | bytes accessed | tf_op | source)
XLA Modules:
  0.0 544.8 jit_solution(254540807391050229)
XLA Ops:
  1.3 1.9 slice_bitcast_fusion.1.x_ref.x4_ref
  5.7 5.7 %copy.71 = bf16[768,2304]{0,1:T(8,128)(2,1)} copy(bf16[768,2304]{1,0:T(8,128)(2,1)} %w_ref.3) | data formatting | bytes 7077888 | tf_op args[5]
  11.4 2.2 copy.72
  13.7 3.7 copy.73.w_ref
  20.9 5.6 %qkv_split.1 = bf16[4,320,576]{2,1,0:T(8,128)(2,1)} custom-call(bf16[320,768]{1,0:T(8,128)(2,1)} %slice_bitcast_fusion.1.x_ref.x4_ref, bf16[320,768]{1,0:T(8,128)(2,1)} %convolution_convert_fusion.pe_ref, f32[1,768]{1,0:T(1,128)} %reshape.245.g_ref, f32[1,768]{1,0:T(1,128)} %reshape.247.b_ref, bf16[4,768,576]{2,1,0:T(8,128)(2,1)} %copy.73.w_ref, ...), custom_call_target="tpu_custom_call" | custom-call | flops 1132462080 | bytes 5013504 | tf_op jit(solution)/shard_map/qkv_split/pallas_call | solution.py:97
  26.5 4.5 all-to-all-start.2
  34.5 17.9 %all-to-all-done.2 = bf16[4,320,576]{2,1,0:T(8,128)(2,1)} async-done(((bf16[4,320,576]{2,1,0:T(8,128)(2,1)}), bf16[4,320,576]{2,1,0:T(8,128)(2,1)}, u32[]{:S(2)}, u32[]{:S(2)}) %all-to-all-start.2) | async-done | bytes 1474592 | tf_op jit(solution)/shard_map/all_to_all | solution.py:803
  52.5 4.4 all-to-all-start
  66.2 10.5 %attend_split.1 = (bf16[1280,192]{1,0:T(8,128)(2,1)}, f32[8,1280]{1,0:T(8,128)}) custom-call(bf16[1280,576]{1,0:T(8,128)(2,1)} %bitcast.9.qkv_ref, f32[1280,256]{1,0:T(8,128)} %broadcast_in_dim.40.kb_ref), custom_call_target="tpu_custom_call" | custom-call | flops 6039797760 | bytes 5898240 | tf_op jit(solution)/shard_map/attend_split/pallas_call | solution.py:204
  76.7 2.2 copy.75
  78.9 2.3 all-to-all-done
  81.2 3.5 all-to-all-start.3
  84.7 9.9 %qkv_whole.1.q_ref.k_ref.v_ref = bf16[1280,2304]{1,0:T(8,128)(2,1)} custom-call(bf16[1280,768]{1,0:T(8,128)(2,1)} %bitcast.x_ref.xm_ref, bf16[320,768]{1,0:T(8,128)(2,1)} %convolution_convert_fusion.pe_ref, f32[1,768]{1,0:T(1,128)} %reshape.245.g_ref, f32[1,768]{1,0:T(1,128)} %reshape.247.b_ref, bf16[768,2304]{1,0:T(8,128)(2,1)} %w_ref.3, ...), custom_call_target="tpu_custom_call" | custom-call | flops 4529848320 | bytes 11403264 | tf_op jit(solution)/shard_map/qkv_whole/pallas_call | solution.py:65
  94.6 4.8 all-to-all-start.1
  101.8 34.3 %attend_whole.1 = (bf16[1280,768]{1,0:T(8,128)(2,1)}, f32[6,8,1280]{2,1,0:T(8,128)}) custom-call(bf16[1280,2304]{1,0:T(8,128)(2,1)} %qkv_whole.1.q_ref.k_ref.v_ref, bf16[1280,2304]{1,0:T(8,128)(2,1)} %qkv_whole.1.q_ref.k_ref.v_ref, bf16[1280,2304]{1,0:T(8,128)(2,1)} %qkv_whole.1.q_ref.k_ref.v_ref, f32[1280,256]{1,0:T(8,128)} %broadcast_in_dim.38.kb_ref), custom_call_target="tpu_custom_call" | custom-call | flops 24159191040 | bytes 7864320 | tf_op jit(solution)/shard_map/attend_whole/pallas_call | solution.py:166
  136.2 94.6 %mlp.1 = (bf16[1280,768]{1,0:T(8,128)(2,1)}, f32[320,768]{1,0:T(8,128)}, bf16[1280,768]{1,0:T(8,128)(2,1)}, bf16[320,768]{1,0:T(8,128)(2,1)}, bf16[1280,768]{1,0...) custom-call(bf16[1280,768]{1,0:T(8,128)(2,1)} %bitcast.x_ref.xm_ref,, ...), custom_call_target="tpu_custom_call" | custom-call | flops 50960793600 | bytes 19660800 | tf_op jit(solution)/shard_map/mlp/pallas_call | solution.py:563
  232.9 2.2 copy.78
  235.1 3.5 all-to-all-start.5
  238.9 2.4 collective-permute-start.11
  241.3 4.5 constant_dynamic-slice_fusion.1
  253.3 2.6 collective-permute-start.12
  256.0 12.9 %back_split.1 = bf16[1280,576]{1,0:T(8,128)(2,1)} custom-call(bf16[1280,576]{1,0:T(8,128)(2,1)} %bitcast.9.qkv_ref, bf16[1280,192]{1,0:T(8,128)(2,1)} %bitcast.161, bf16[1280,192]{1,0:T(8,128)(2,1)} %get-tuple-element.37.o_ref, f32[8,1280]{1,0:T(8,128)} %get-tuple-element.45.lse_ref, f32[1280,256]{1,0:T(8,128)} %broadcast_in_dim.40.kb_ref), custom_call_target="tpu_custom_call" | custom-call | flops 15099494400 | bytes 5898240 | tf_op jit(solution)/shard_map/back_split/pallas_call | solution.py:359
  268.8 3.9 all-to-all-start.6
  275.4 39.6 %back_whole.1.dm_ref = bf16[3,1280,768]{2,1,0:T(8,128)(2,1)} custom-call(bf16[1280,2304]{1,0:T(8,128)(2,1)} %qkv_whole.1.q_ref.k_ref.v_ref, bf16[1280,2304]{1,0:T(8,128)(2,1)} %qkv_whole.1.q_ref.k_ref.v_ref, bf16[1280,2304]{1,0:T(8,128)(2,1)} %qkv_whole.1.q_ref.k_ref.v_ref, bf16[1280,768]{1,0:T(8,128)(2,1)} %get-tuple-element.42.do_ref, ...), custom_call_target="tpu_custom_call" | custom-call | flops 60397977600 | bytes 15728640 | tf_op jit(solution)/shard_map/back_whole/pallas_call | solution.py:286
  315.1 39.6 %all-reduce = (f32[8,768]{1,0:T(8,128)}, f32[3072]{0:T(1024)}) all-reduce(f32[8,768]{1,0:T(8,128)S(1)} %copy-done.15, f32[3072]{0:T(1024)S(1)} %bitcast.163), channel_id=1, replica_groups=mesh['dp'=8,'mix'=4] {'dp','mix'}, use_global_device_ids=true, to_apply=%region_0.1 | all-reduce | flops 9216 | bytes 73728 | tf_op jit(solution)/shard_map/psum | solution.py:847
  357.4 3.8 all-to-all-start.4
  361.3 17.7 %input_grad.1 = (bf16[1280,768]{1,0:T(8,128)(2,1)}, f32[320,768]{1,0:T(8,128)}, f32[16,768]{1,0:T(8,128)}) custom-call(bf16[1280,768]{1,0:T(8,128)(2,1)} %bitcast.x_ref.xm_ref, bf16[320,768]{1,0:T(8,128)(2,1)} %slice_bitcast_fusion.1.x_ref.x4_ref, bf16[320,768]{1,0:T(8,128)(2,1)} %convolution_convert_fusion.pe_ref, f32[1,768]{1,0:T(1,128)} %reshape.245.g_ref, ...), custom_call_target="tpu_custom_call" | custom-call | flops 5662310400 | bytes 13369344 | tf_op jit(solution)/shard_map/input_grad/pallas_call | solution.py:700
  380.5 14.6 %wqkv_grad.1 = (bf16[4,768,576]{2,1,0:T(8,128)(2,1)}, f32[1,2304]{1,0:T(1,128)}) custom-call(bf16[1280,768]{1,0:T(8,128)(2,1)} %bitcast.x_ref.xm_ref, bf16[320,768]{1,0:T(8,128)(2,1)} %slice_bitcast_fusion.1.x_ref.x4_ref, bf16[320,768]{1,0:T(8,128)(2,1)} %convolution_convert_fusion.pe_ref, f32[1,768]{1,0:T(1,128)} %reshape.245.g_ref, ...), custom_call_target="tpu_custom_call" | custom-call | flops 5662310400 | bytes 13369344 | tf_op jit(solution)/shard_map/wqkv_grad/pallas_call | solution.py:646
  397.2 1.8 collective-permute-start.14
  399.5 3.8 constant_dynamic-slice_fusion.7
  404.9 2.2 collective-permute-start.2
  411.1 4.7 all-to-all-start.7
  418.2 2.3 fusion
  422.4 2.4 fusion.1
  427.6 2.6 pad_maximum_fusion
  431.5 8.6 %all-to-all-done.7 = bf16[4,320,768]{2,1,0:T(8,128)(2,1)} async-done(((bf16[4,320,768]{2,1,0:T(8,128)(2,1)}), bf16[4,320,768]{2,1,0:T(8,128)(2,1)}, u32[]{:S(2)}, u32[]{:S(2)}) %all-to-all-start.7) | async-done | bytes 1966112 | tf_op jit(solution)/shard_map/all_to_all | solution.py:803
  440.1 2.0 convert_element_type.262
  442.3 2.0 fusion.2
  446.2 29.0 %collective-permute-done.21 = bf16[2,2,2,192,384]{4,3,0,2,1:T(8,128)(2,1)} collective-permute-done((bf16[2,2,2,192,384]{4,3,0,2,1:T(8,128)(2,1)S(1)}, bf16[2,2,2,192,384]{4,3,0,2,1:T(8,128)(2,1)}, u32[]{:S(2)}, u32[]{:S(2)}) %collective-permute-start.21) | collective-permute-done | bytes 1179680 | tf_op jit(solution)/shard_map/ppermute | solution.py:715
  478.8 2.1 collective-permute-start.17
  480.9 2.6 pad_maximum_fusion.1
  483.5 18.2 %collective-permute-done.22 = bf16[2,2,192,384]{3,2,0,1:T(8,128)(2,1)S(1)} collective-permute-done((bf16[2,2,192,384]{3,2,0,1:T(8,128)(2,1)S(1)}, bf16[2,2,192,384]{3,2,0,1:T(8,128)(2,1)S(1)}, u32[]{:S(2)}, u32[]{:S(2)}) %collective-permute-start.22) | collective-permute-done | bytes 589856 | tf_op jit(solution)/shard_map/ppermute | solution.py:715
  503.7 4.0 collective-permute-done.17
  508.3 2.0 collective-permute-start.7
  512.1 8.5 %collective-permute-done.18 = bf16[2,96,768]{2,1,0:T(8,128)(2,1)S(1)} collective-permute-done((bf16[2,96,768]{2,1,0:T(8,128)(2,1)S(1)}, bf16[2,96,768]{2,1,0:T(8,128)(2,1)S(1)}, u32[]{:S(2)}, u32[]{:S(2)}) %collective-permute-start.18) | collective-permute-done | bytes 294944 | tf_op jit(solution)/shard_map/ppermute | solution.py:715
  522.4 9.7 %collective-permute-done.7 = bf16[2,2,96,576]{3,2,0,1:T(8,128)(2,1)S(1)} collective-permute-done((bf16[2,2,96,576]{3,2,0,1:T(8,128)(2,1)S(1)}, bf16[2,2,96,576]{3,2,0,1:T(8,128)(2,1)S(1)}, u32[]{:S(2)}, u32[]{:S(2)}) %collective-permute-start.7) | collective-permute-done | bytes 442400 | tf_op jit(solution)/shard_map/ppermute | solution.py:715
  533.1 5.4 collective-permute-done.8
  541.1 2.5 collective-permute-done.9
  (185 shorter events, 71.0 us)
Async XLA Ops:
  0.6 19.1 %copy-start = (bf16[5,768]{1,0:T(8,128)(2,1)S(1)}, bf16[5,768]{1,0:T(8,128)(2,1)}, u32[]{:S(2)}) copy-start(bf16[5,768]{1,0:T(8,128)(2,1)} %param.19) | copy-start | bytes 23044
  26.5 4.6 copy-start.7
  26.5 26.0 %all-to-all-start.2 = ((bf16[4,320,576]{2,1,0:T(8,128)(2,1)}), bf16[4,320,576]{2,1,0:T(8,128)(2,1)}, u32[]{:S(2)}, u32[]{:S(2)}) async-start(bf16[4,320,576]{2,1,0:T(8,128)(2,1)} %qkv_split.1), calls=%async_computation.2 | async-start | bytes 3276800 | tf_op jit(solution)/shard_map/all_to_all | solution.py:803
  32.5 25.3 %copy-start.8 = (bf16[5,320,768]{2,1,0:T(8,128)(2,1)S(1)}, bf16[5,320,768]{2,1,0:T(8,128)(2,1)}, u32[]{:S(2)}) copy-start(bf16[5,320,768]{2,1,0:T(8,128)(2,1)} %param.33) | copy-start | bytes 7372804
  52.5 28.8 %all-to-all-start = ((bf16[4,320,768]{2,1,0:T(8,128)(2,1)}), bf16[4,320,768]{2,1,0:T(8,128)(2,1)}, u32[]{:S(2)}, u32[]{:S(2)}) async-start(bf16[4,320,768]{2,1,0:T(8,128)(2,1)} %slice.51), calls=%async_computation | async-start | bytes 3932160 | tf_op jit(solution)/shard_map/all_to_all | solution.py:803
  57.0 4.0 copy-start.23
  57.0 4.6 copy-start.24
  81.2 13.3 %all-to-all-start.3 = ((bf16[4,320,192]{1,2,0:T(8,128)(2,1)}), bf16[4,320,192]{1,2,0:T(8,128)(2,1)S(1)}, u32[]{:S(2)}, u32[]{:S(2)}) async-start(bf16[4,320,192]{1,2,0:T(8,128)(2,1)} %copy.75), calls=%async_computation.3 | async-start | bytes 1179648 | tf_op jit(solution)/shard_map/all_to_all | solution.py:803
  94.6 41.6 %all-to-all-start.1 = ((bf16[4,320,768]{2,1,0:T(8,128)(2,1)}), bf16[4,320,768]{2,1,0:T(8,128)(2,1)}, u32[]{:S(2)}, u32[]{:S(2)}) async-start(bf16[4,320,768]{2,1,0:T(8,128)(2,1)} %slice.53), calls=%async_computation.1 | async-start | bytes 3932160 | tf_op jit(solution)/shard_map/all_to_all | solution.py:803
  232.4 6.2 %collective-permute-start.10 = (bf16[2,2,2,2,96,192]{5,4,0,2,1,3:T(8,128)(2,1)S(1)}, bf16[2,2,2,2,96,192]{5,4,0,2,1,3:T(8,128)(2,1)S(1)}, u32[]{:S(2)}, u32[]{:S(2)}) collective-permute-start(bf16[2,2,2,2,96,192]{5,4,0,2,1,3:T(8,128)(2,1)S(1)} %bitcast.159), channel_id=1, source_target_pairs={{0,1},{1,0},{2,3},{3,2},{4,5},{5,4},{6,7},{7,6},{8,9},{9,8},{10,11... | collective-permute-start | bytes 1769480 | tf_op jit(solution)/shard_map/ppermute | solution.py:715
  235.1 16.2 %all-to-all-start.5 = ((bf16[4,320,192]{1,2,0:T(8,128)(2,1)}), bf16[4,320,192]{1,2,0:T(8,128)(2,1)S(1)}, u32[]{:S(2)}, u32[]{:S(2)}) async-start(bf16[4,320,192]{1,2,0:T(8,128)(2,1)} %copy.78), calls=%async_computation.5 | async-start | bytes 1179648 | tf_op jit(solution)/shard_map/all_to_all | solution.py:803
  238.9 13.6 %collective-permute-start.11 = (bf16[2,2,2,96,192]{4,3,0,2,1:T(8,128)(2,1)S(1)}, bf16[2,2,2,96,192]{4,3,0,2,1:T(8,128)(2,1)S(1)}, u32[]{:S(2)}, u32[]{:S(2)}) collective-permute-start(bf16[2,2,2,96,192]{4,3,0,2,1:T(8,128)(2,1)S(1)} %dynamic-slice_bitcast_fusion.6), channel_id=1, source_target_pairs={{0,4},{4,0},{8,12},{12,8},{16,20},{20,16},{24,28},{28,24},{1,5},{5... | collective-permute-start | bytes 884744 | tf_op jit(solution)/shard_map/ppermute | solution.py:715
  241.3 6.4 %slice-start = ((s8[4718592]{0:T(1024)(128)(4,1)}), s8[4194304]{0:T(1024)(128)(4,1)S(1)}, s32[]{:S(2)}) async-start(s8[4718592]{0:T(1024)(128)(4,1)} %bitcast.148), calls=%async_computation.8 | async-start | bytes 8388608
  241.3 6.4 %slice-start.1 = ((s8[4718592]{0:T(1024)(128)(4,1)}), s8[524288]{0:T(1024)(128)(4,1)S(1)}, s32[]{:S(2)}) async-start(s8[4718592]{0:T(1024)(128)(4,1)} %bitcast.148), calls=%async_computation.9 | async-start | bytes 1048576
  247.5 170.1 %collective-permute-start.20 = (bf16[2,2,2,2,192,384]{5,4,0,3,2,1:T(8,128)(2,1)}, bf16[2,2,2,2,192,384]{5,4,0,3,2,1:T(8,128)(2,1)}, u32[]{:S(2)}, u32[]{:S(2)}) collective-permute-start(bf16[2,2,2,2,192,384]{5,4,0,3,2,1:T(8,128)(2,1)} %bitcast.142), channel_id=1, source_target_pairs={{0,1},{1,0},{2,3},{3,2},{4,5},{5,4},{6,7},{7,6},{8,9},{9,8},{10,11... | collective-permute-start | bytes 7077896 | tf_op jit(solution)/shard_map/ppermute | solution.py:715
  251.0 171.4 %collective-permute-start.15 = (bf16[2,2,2,2,96,768]{5,4,0,2,1,3:T(8,128)(2,1)}, bf16[2,2,2,2,96,768]{5,4,0,2,1,3:T(8,128)(2,1)}, u32[]{:S(2)}, u32[]{:S(2)}) collective-permute-start(bf16[2,2,2,2,96,768]{5,4,0,2,1,3:T(8,128)(2,1)} %bitcast.143), channel_id=1, source_target_pairs={{0,1},{1,0},{2,3},{3,2},{4,5},{5,4},{6,7},{7,6},{8,9},{9,8},{10,11... | collective-permute-start | bytes 7077896 | tf_op jit(solution)/shard_map/ppermute | solution.py:715
  253.3 19.4 %collective-permute-start.12 = (bf16[2,2,96,192]{3,2,0,1:T(8,128)(2,1)S(1)}, bf16[2,2,96,192]{3,2,0,1:T(8,128)(2,1)}, u32[]{:S(2)}, u32[]{:S(2)}) collective-permute-start(bf16[2,2,96,192]{3,2,0,1:T(8,128)(2,1)S(1)} %dynamic-slice_bitcast_fusion.10), channel_id=1, source_target_pairs={{0,16},{4,20},{8,24},{12,28},{16,0},{20,4},{24,8},{28,12},{1,17},{... | collective-permute-start | bytes 442376 | tf_op jit(solution)/shard_map/ppermute | solution.py:715
  268.8 3.9 copy-start.11
  268.8 87.4 %all-to-all-start.6 = ((bf16[4,320,576]{2,1,0:T(8,128)(2,1)}), bf16[4,320,576]{2,1,0:T(8,128)(2,1)S(1)}, u32[]{:S(2)}, u32[]{:S(2)}) async-start(bf16[4,320,576]{2,1,0:T(8,128)(2,1)} %bitcast.155), calls=%async_computation.6 | async-start | bytes 3276800 | tf_op jit(solution)/shard_map/all_to_all | solution.py:803
  273.8 80.9 %collective-permute-start.13 = (bf16[2,96,192]{2,1,0:T(8,128)(2,1)S(1)}, bf16[2,96,192]{2,1,0:T(8,128)(2,1)}, u32[]{:S(2)}, u32[]{:S(2)}) collective-permute-start(bf16[2,96,192]{2,1,0:T(8,128)(2,1)S(1)} %dynamic-slice_bitcast_fusion.14), channel_id=1, source_target_pairs={{0,8},{4,12},{8,0},{12,4},{16,24},{20,28},{24,16},{28,20},{1,9},{5... | collective-permute-start | bytes 221192 | tf_op jit(solution)/shard_map/ppermute | solution.py:715
  275.4 39.6 %copy-start.15 = (f32[8,768]{1,0:T(8,128)S(1)}, f32[8,768]{1,0:T(8,128)}, u32[]{:S(2)}) copy-start(f32[8,768]{1,0:T(8,128)} %get-tuple-element.52) | copy-start | bytes 73732
  275.4 39.6 %copy-start.16 = (f32[8,1,384]{2,1,0:T(1,128)S(1)}, f32[8,1,384]{2,1,0:T(1,128)}, u32[]{:S(2)}) copy-start(f32[8,1,384]{2,1,0:T(1,128)} %get-tuple-element.54) | copy-start | bytes 36868
  357.4 53.6 %all-to-all-start.4 = ((bf16[4,320,768]{2,1,0:T(8,128)(2,1)}), bf16[4,320,768]{2,1,0:T(8,128)(2,1)S(1)}, u32[]{:S(2)}, u32[]{:S(2)}) async-start(bf16[4,320,768]{2,1,0:T(8,128)(2,1)} %bitcast.153), calls=%async_computation.4 | async-start | bytes 3932160 | tf_op jit(solution)/shard_map/all_to_all | solution.py:803
  395.8 3.2 collective-permute-start
  397.2 18.7 %collective-permute-start.14 = (bf16[96,192]{1,0:T(8,128)(2,1)S(1)}, bf16[96,192]{1,0:T(8,128)(2,1)S(1)}, u32[]{:S(2)}, u32[]{:S(2)}) collective-permute-start(bf16[96,192]{1,0:T(8,128)(2,1)S(1)} %dynamic-slice_bitcast_fusion.15), channel_id=1, source_target_pairs={{0,2},{1,3},{2,0},{3,1},{4,6},{5,7},{6,4},{7,5},{8,10},{9,11},{10,... | collective-permute-start | bytes 110600 | tf_op jit(solution)/shard_map/ppermute | solution.py:715
  399.0 5.9 %collective-permute-start.1 = (f32[10,768]{1,0:T(8,128)S(1)}, f32[10,768]{1,0:T(8,128)S(1)}, u32[]{:S(2)}, u32[]{:S(2)}) collective-permute-start(f32[10,768]{1,0:T(8,128)S(1)} %fusion.30), channel_id=1, source_target_pairs={{0,2},{1,3},{2,0},{3,1},{4,6},{5,7},{6,4},{7,5},{8,10},{9,11},{10,... | collective-permute-start | bytes 92168 | tf_op jit(solution)/shard_map/ppermute | solution.py:715
  404.9 11.0 %copy-start.14 = (bf16[2,96,192]{2,1,0:T(8,128)(2,1)S(1)}, bf16[2,96,192]{2,1,0:T(8,128)(2,1)}, u32[]{:S(2)}) copy-start(bf16[2,96,192]{2,1,0:T(8,128)(2,1)} %fusion.16) | copy-start | bytes 221188
  404.9 37.3 %collective-permute-start.5 = (bf16[2,2,2,2,96,576]{5,4,0,2,1,3:T(8,128)(2,1)}, bf16[2,2,2,2,96,576]{5,4,0,2,1,3:T(8,128)(2,1)}, u32[]{:S(2)}, u32[]{:S(2)}) collective-permute-start(bf16[2,2,2,2,96,576]{5,4,0,2,1,3:T(8,128)(2,1)} %bitcast.144), channel_id=1, source_target_pairs={{0,1},{1,0},{2,3},{3,2},{4,5},{5,4},{6,7},{7,6},{8,9},{9,8},{10,11... | collective-permute-start | bytes 5308424 | tf_op jit(solution)/shard_map/ppermute | solution.py:715
  404.9 4.6 collective-permute-start.2
  409.4 7.4 %collective-permute-start.3 = (f32[10,768]{1,0:T(8,128)S(1)}, f32[10,768]{1,0:T(8,128)S(1)}, u32[]{:S(2)}, u32[]{:S(2)}) collective-permute-start(f32[10,768]{1,0:T(8,128)S(1)} %add.252), channel_id=1, source_target_pairs={{0,8},{4,12},{8,0},{12,4},{16,24},{20,28},{24,16},{28,20},{1,9},{5... | collective-permute-start | bytes 92168 | tf_op jit(solution)/shard_map/ppermute | solution.py:715
  411.1 29.0 %all-to-all-start.7 = ((bf16[4,320,768]{2,1,0:T(8,128)(2,1)}), bf16[4,320,768]{2,1,0:T(8,128)(2,1)}, u32[]{:S(2)}, u32[]{:S(2)}) async-start(bf16[4,320,768]{2,1,0:T(8,128)(2,1)} %bitcast.154), calls=%async_computation.7 | async-start | bytes 3932160 | tf_op jit(solution)/shard_map/all_to_all | solution.py:803
  416.9 13.4 %collective-permute-start.4 = (f32[10,768]{1,0:T(8,128)S(1)}, f32[10,768]{1,0:T(8,128)S(1)}, u32[]{:S(2)}, u32[]{:S(2)}) collective-permute-start(f32[10,768]{1,0:T(8,128)S(1)} %add.253), channel_id=1, source_target_pairs={{0,16},{4,20},{8,24},{12,28},{16,0},{20,4},{24,8},{28,12},{1,17},{... | collective-permute-start | bytes 92168 | tf_op jit(solution)/shard_map/ppermute | solution.py:715
  420.6 54.7 %collective-permute-start.21 = (bf16[2,2,2,192,384]{4,3,0,2,1:T(8,128)(2,1)S(1)}, bf16[2,2,2,192,384]{4,3,0,2,1:T(8,128)(2,1)}, u32[]{:S(2)}, u32[]{:S(2)}) collective-permute-start(bf16[2,2,2,192,384]{4,3,0,2,1:T(8,128)(2,1)S(1)} %dynamic-slice_bitcast_fusion), channel_id=1, source_target_pairs={{0,16},{4,20},{8,24},{12,28},{16,0},{20,4},{24,8},{28,12},{1,17},{... | collective-permute-start | bytes 3538952 | tf_op jit(solution)/shard_map/ppermute | solution.py:715
  424.8 5.5 %copy-start.4 = (bf16[2,2,2,2,96,768]{5,4,0,2,1,3:T(8,128)(2,1)}, bf16[2,2,2,2,96,768]{5,4,0,2,1,3:T(8,128)(2,1)S(1)}, u32[]{:S(2)}) copy-start(bf16[2,2,2,2,96,768]{5,4,0,2,1,3:T(8,128)(2,1)S(1)} %fusion.1) | copy-start | bytes 7077892
  425.9 51.2 %collective-permute-start.16 = (bf16[2,2,2,96,768]{4,3,0,2,1:T(8,128)(2,1)}, bf16[2,2,2,96,768]{4,3,0,2,1:T(8,128)(2,1)}, u32[]{:S(2)}, u32[]{:S(2)}) collective-permute-start(bf16[2,2,2,96,768]{4,3,0,2,1:T(8,128)(2,1)} %dynamic-slice_bitcast_fusion.1), channel_id=1, source_target_pairs={{0,4},{4,0},{8,12},{12,8},{16,20},{20,16},{24,28},{28,24},{1,5},{5... | collective-permute-start | bytes 3538952 | tf_op jit(solution)/shard_map/ppermute | solution.py:715
  444.4 32.7 %copy-start.5 = (bf16[2,2,2,2,96,768]{5,4,0,2,1,3:T(8,128)(2,1)S(1)}, bf16[2,2,2,2,96,768]{5,4,0,2,1,3:T(8,128)(2,1)}, u32[]{:S(2)}) copy-start(bf16[2,2,2,2,96,768]{5,4,0,2,1,3:T(8,128)(2,1)} %copy-done.4) | copy-start | bytes 7077892
  444.4 63.5 %collective-permute-start.6 = (bf16[2,2,2,96,576]{4,3,0,2,1:T(8,128)(2,1)S(1)}, bf16[2,2,2,96,576]{4,3,0,2,1:T(8,128)(2,1)S(1)}, u32[]{:S(2)}, u32[]{:S(2)}) collective-permute-start(bf16[2,2,2,96,576]{4,3,0,2,1:T(8,128)(2,1)S(1)} %dynamic-slice_bitcast_fusion.2), channel_id=1, source_target_pairs={{0,4},{4,0},{8,12},{12,8},{16,20},{20,16},{24,28},{28,24},{1,5},{5... | collective-permute-start | bytes 2654216 | tf_op jit(solution)/shard_map/ppermute | solution.py:715
  477.0 3.9 copy-start.13
  477.0 24.7 %collective-permute-start.22 = (bf16[2,2,192,384]{3,2,0,1:T(8,128)(2,1)S(1)}, bf16[2,2,192,384]{3,2,0,1:T(8,128)(2,1)S(1)}, u32[]{:S(2)}, u32[]{:S(2)}) collective-permute-start(bf16[2,2,192,384]{3,2,0,1:T(8,128)(2,1)S(1)} %dynamic-slice_bitcast_fusion.3), channel_id=1, source_target_pairs={{0,8},{4,12},{8,0},{12,4},{16,24},{20,28},{24,16},{28,20},{1,9},{5... | collective-permute-start | bytes 1769480 | tf_op jit(solution)/shard_map/ppermute | solution.py:715
  478.8 28.9 %collective-permute-start.17 = (bf16[2,2,96,768]{3,2,0,1:T(8,128)(2,1)S(1)}, bf16[2,2,96,768]{3,2,0,1:T(8,128)(2,1)S(1)}, u32[]{:S(2)}, u32[]{:S(2)}) collective-permute-start(bf16[2,2,96,768]{3,2,0,1:T(8,128)(2,1)S(1)} %dynamic-slice_bitcast_fusion.4), channel_id=1, source_target_pairs={{0,16},{4,20},{8,24},{12,28},{16,0},{20,4},{24,8},{28,12},{1,17},{... | collective-permute-start | bytes 1769480 | tf_op jit(solution)/shard_map/ppermute | solution.py:715
  501.9 8.4 %collective-permute-start.23 = (bf16[2,192,384]{2,1,0:T(8,128)(2,1)S(1)}, bf16[2,192,384]{2,1,0:T(8,128)(2,1)S(1)}, u32[]{:S(2)}, u32[]{:S(2)}) collective-permute-start(bf16[2,192,384]{2,1,0:T(8,128)(2,1)S(1)} %dynamic-slice_bitcast_fusion.7), channel_id=1, source_target_pairs={{0,4},{4,0},{8,12},{12,8},{16,20},{20,16},{24,28},{28,24},{1,5},{5... | collective-permute-start | bytes 884744 | tf_op jit(solution)/shard_map/ppermute | solution.py:715
  507.9 12.7 %collective-permute-start.18 = (bf16[2,96,768]{2,1,0:T(8,128)(2,1)S(1)}, bf16[2,96,768]{2,1,0:T(8,128)(2,1)S(1)}, u32[]{:S(2)}, u32[]{:S(2)}) collective-permute-start(bf16[2,96,768]{2,1,0:T(8,128)(2,1)S(1)} %dynamic-slice_bitcast_fusion.8), channel_id=1, source_target_pairs={{0,8},{4,12},{8,0},{12,4},{16,24},{20,28},{24,16},{28,20},{1,9},{5... | collective-permute-start | bytes 884744 | tf_op jit(solution)/shard_map/ppermute | solution.py:715
  508.3 23.8 %collective-permute-start.7 = (bf16[2,2,96,576]{3,2,0,1:T(8,128)(2,1)S(1)}, bf16[2,2,96,576]{3,2,0,1:T(8,128)(2,1)S(1)}, u32[]{:S(2)}, u32[]{:S(2)}) collective-permute-start(bf16[2,2,96,576]{3,2,0,1:T(8,128)(2,1)S(1)} %dynamic-slice_bitcast_fusion.5), channel_id=1, source_target_pairs={{0,16},{4,20},{8,24},{12,28},{16,0},{20,4},{24,8},{28,12},{1,17},{... | collective-permute-start | bytes 1327112 | tf_op jit(solution)/shard_map/ppermute | solution.py:715
  510.4 22.0 %collective-permute-start.24 = (bf16[192,384]{1,0:T(8,128)(2,1)S(1)}, bf16[192,384]{1,0:T(8,128)(2,1)S(1)}, u32[]{:S(2)}, u32[]{:S(2)}) collective-permute-start(bf16[192,384]{1,0:T(8,128)(2,1)S(1)} %dynamic-slice_bitcast_fusion.11), channel_id=1, source_target_pairs={{0,2},{1,3},{2,0},{3,1},{4,6},{5,7},{6,4},{7,5},{8,10},{9,11},{10,... | collective-permute-start | bytes 442376 | tf_op jit(solution)/shard_map/ppermute | solution.py:715
  520.7 23.7 %copy-start.1 = (bf16[5,768]{1,0:T(8,128)(2,1)S(1)}, bf16[5,768]{1,0:T(8,128)(2,1)}, u32[]{:S(2)}) copy-start(bf16[5,768]{1,0:T(8,128)(2,1)} %param.19) | copy-start | bytes 23044
  520.7 19.7 %collective-permute-start.19 = (bf16[96,768]{1,0:T(8,128)(2,1)S(1)}, bf16[96,768]{1,0:T(8,128)(2,1)S(1)}, u32[]{:S(2)}, u32[]{:S(2)}) collective-permute-start(bf16[96,768]{1,0:T(8,128)(2,1)S(1)} %dynamic-slice_bitcast_fusion.12), channel_id=1, source_target_pairs={{0,2},{1,3},{2,0},{3,1},{4,6},{5,7},{6,4},{7,5},{8,10},{9,11},{10,... | collective-permute-start | bytes 442376 | tf_op jit(solution)/shard_map/ppermute | solution.py:715
  532.3 6.3 %collective-permute-start.8 = (bf16[2,96,576]{2,1,0:T(8,128)(2,1)S(1)}, bf16[2,96,576]{2,1,0:T(8,128)(2,1)S(1)}, u32[]{:S(2)}, u32[]{:S(2)}) collective-permute-start(bf16[2,96,576]{2,1,0:T(8,128)(2,1)S(1)} %dynamic-slice_bitcast_fusion.9), channel_id=1, source_target_pairs={{0,8},{4,12},{8,0},{12,4},{16,24},{20,28},{24,16},{28,20},{1,9},{5... | collective-permute-start | bytes 663560 | tf_op jit(solution)/shard_map/ppermute | solution.py:715
  538.7 4.9 collective-permute-start.9
  (13 other events, 27.4 us)
